TPU v7x, 256 devices: a whole 4x4x8 slice. The times are simulated.
256 devices in a mesh: sector: 32 (over y_hi, z, core), col: 8 (over x, y_lo).
Axes of the slice: x: 4, y: 4 (y_hi: 2, y_lo: 2; y = y_hi * 2 + y_lo), z: 8, core: 2. Of those that a mesh axis runs over, the one named last changes fastest.
Arguments:
- prev_nodes: float32 [4, 2, 512, 128, 256], P(None, None, 'col', 'sector'), may hold values from -6 to 6
- stiffness: float32 [128, 256], P('sector'), may hold values from 1 to 4
- aero_coef: bfloat16 [32, 128, 128], replicated, may hold values from -0.125 to 0.125
- offset_slot: int32 [128], replicated, may hold values from 0 to 31
- contact_left: int32 [128, 128], P('sector'), may hold values from 0 to 255
- contact_right: int32 [128, 128], P('sector'), may hold values from 0 to 255
- contact_mask: int32 [128, 128], P('sector'), may hold values from 0 to 2
Outputs:
- scaled_end: float32 [2, 512, 128, 256], P(None, 'col', 'sector')
- growth: float32 [], replicated
All inputs are finite; a program needn't handle non-finite values.
Results may differ from a plain program's by a relative error of at most 0.0012.
Values may be sent and summed in bfloat16 or wider, within the bound.
A program may use at most 128 MiB of HBM per device.

v0:
```python
import functools
import math

import jax
import jax.numpy as jnp
from jax import lax
from jax.experimental import pallas as pl
from jax.experimental.pallas import tpu as pltpu
from jax.sharding import PartitionSpec as P

DOF = 256
AERO = 128
TABLES = 32
LOCAL = 4
MESH = pl.DeviceIdType.MESH
F32 = jnp.float32
BF16 = jnp.bfloat16

time_step = 0.25
coupling = 0.5
damping = 0.1
k_stick = 4.0
k_slip = 1.0


def quad_tables():
    root = 1.0 / math.sqrt(5.0)
    tau = [0.0, (1.0 - root) / 2.0, (1.0 + root) / 2.0, 1.0]
    table = []
    for m in range(3):
        table_row = []
        for j in range(4):
            coeffs = [1.0]
            scale = 1.0
            for k in range(4):
                if k != j:
                    widened = [0.0] * (len(coeffs) + 1)
                    for power in range(len(coeffs)):
                        widened[power + 1] = widened[power + 1] + coeffs[power]
                        widened[power] = widened[power] - tau[k] * coeffs[power]
                    coeffs = widened
                    scale = scale * (tau[j] - tau[k])
            integral = 0.0
            for power in range(len(coeffs)):
                integral = integral + coeffs[power] * (
                    tau[m + 1] ** (power + 1) - tau[m] ** (power + 1)
                ) / (power + 1)
            table_row.append(integral / scale * time_step)
        table.append(table_row)
    steps = [(tau[m + 1] - tau[m]) * time_step for m in range(3)]
    return (table, steps)


S, H = quad_tables()
H1, H2 = H[1], H[2]
C1 = (1.0 - damping * H1) * (1.0 - damping * H2)
C2 = 1.0 - damping * H2
C3 = H1 + H2 * (1.0 - damping * H1)
HH = H1 * H2


def swap_halves(a, b):
    axis = a.ndim - 2
    low = lax.broadcasted_iota(jnp.int32, a.shape, axis) < 4
    return (
        jnp.where(low, a, pltpu.roll(b, 4, axis)),
        jnp.where(low, pltpu.roll(a, 4, axis), b),
    )


def low_of_pairs(rows):
    tiles = rows.reshape(rows.shape[0] // 16, 2, 8, 128)
    return swap_halves(tiles[:, 0], tiles[:, 1])[0]


def pairs_of_low(chunks):
    low = lax.broadcasted_iota(jnp.int32, chunks.shape, 1) < 4
    first = jnp.where(low, chunks, 0.0)
    second = jnp.where(low, pltpu.roll(chunks, 4, 1), 0.0)
    return jnp.stack([first, second], axis=1).reshape(chunks.shape[0] * 16, 128)


def dot(a, b, dims=(1, 0)):
    return lax.dot_general(
        a, b, (((dims[0],), (dims[1],)), ((), ())), preferred_element_type=F32
    )


def kernel(
    ns, nc, total_count,
    x_hbm, stiff_hbm, coef_hbm, slot_hbm, cl_hbm, cr_hbm, cm_hbm,
    out_hbm, growth_ref,
    xs, stiff, coef, slot, cl, cr, cm, cl_n, cr_n, cm_n,
    keff, mats, smat,
    yp0, yp1, yp2, a0r, halo, cross0, cross1, cross2,
    w_acc, p_acc, e1, e2p, e2w, st,
    send1, rcv1, send2, rcv2, send3, rcv3, send4, rcv4,
    nb_send, nb_rcv, acc1, acc2, part, colsum, secsum, secpart,
    load_sem, small_sem, out_sem,
    int_ssem, int_rsem, nb_ssem, nb_rsem, a_ssem, a_rsem, r_ssem, r_rsem,
):
    me = lax.axis_index("sector")
    mycol = lax.axis_index("col")
    rows = xs.shape[1]
    cols = 2 * ns
    sectors = LOCAL * ns
    block = min(64, rows)
    blocks = rows // block
    nxt = lax.rem(me + 1, ns)
    prv = lax.rem(me + ns - 1, ns)

    barrier = pltpu.get_barrier_semaphore()

    def greet_sector(i, carry):
        pl.semaphore_signal(
            barrier, inc=1, device_id={"sector": lax.rem(me + i, ns)}, device_id_type=MESH
        )
        return carry

    def greet_col(i, carry):
        pl.semaphore_signal(
            barrier, inc=1, device_id={"col": lax.rem(mycol + i, nc)}, device_id_type=MESH
        )
        return carry

    smalls = [
        pltpu.make_async_copy(src, dst, small_sem.at[n])
        for n, (src, dst) in enumerate(
            [(cl_hbm, cl), (cm_hbm, cm), (cr_hbm, cr), (slot_hbm, slot), (stiff_hbm, stiff)]
        )
    ]
    for copy in smalls:
        copy.start()
    loads = [pltpu.make_async_copy(x_hbm.at[n], xs.at[n], load_sem.at[n]) for n in range(8)]
    for copy in loads:
        copy.start()
    coef_load = pltpu.make_async_copy(coef_hbm, coef, load_sem.at[8])
    coef_load.start()
    lax.fori_loop(1, ns, greet_sector, 0)
    lax.fori_loop(1, nc, greet_col, 0)
    for copy in smalls:
        copy.wait()

    smat[...] = pltpu.roll(
        jnp.broadcast_to(slot[...].astype(F32), (sectors, sectors)), 0, 1, stride=1, stride_axis=0
    )

    pl.semaphore_wait(barrier, ns + nc - 2)

    int_copies = [
        pltpu.make_async_remote_copy(
            src, dst, int_ssem.at[n], int_rsem.at[n],
            device_id={"sector": to}, device_id_type=MESH,
        )
        for n, (src, dst, to) in enumerate([(cl, cl_n, nxt), (cm, cm_n, nxt), (cr, cr_n, prv)])
    ]
    for copy in int_copies:
        copy.start()

    for copy in loads:
        copy.wait()

    def combine(i, carry):
        at = pl.ds(pl.multiple_of(i * block, block), block)
        p = [xs[2 * j, at, :] for j in range(4)]
        w = [xs[2 * j + 1, at, :] for j in range(4)]

        def quad(m, v):
            out = v[0] * float(S[m][0])
            for j in range(1, 4):
                out = out + float(S[m][j]) * v[j]
            return out

        y0 = quad(0, p)
        v0 = quad(0, w)
        p1 = p[0] + v0
        y1 = quad(1, p) + H1 * (p1 - p[1])
        yp0[at, :] = y0
        yp1[at, :] = y1
        p_acc[at, :] = p1
        w_acc[at, :] = w[0] - damping * v0
        e1[at, :] = quad(1, w) - H1 * w[1]
        e2p[at, :] = quad(2, p) - H2 * p[2]
        e2w[at, :] = quad(2, w) - H2 * w[2]
        chunk = jnp.concatenate(
            [low_of_pairs(y0), low_of_pairs(C3 * y0 + H2 * y1)], axis=2
        ).astype(BF16)
        per = block // 16
        send1[pl.ds(i * per, per)] = chunk
        return carry

    lax.fori_loop(0, blocks, combine, 0)

    def sector_rows(ref, s):
        return jnp.concatenate(
            [ref[pl.ds(s, cols, stride=8), :], ref[pl.ds(4 + s, cols, stride=8), :]], axis=1
        ).astype(BF16)

    def neighbour_copies(field):
        return [
            pltpu.make_async_remote_copy(
                nb_send.at[side, field], nb_rcv.at[side, field],
                nb_ssem.at[side, field], nb_rsem.at[side, field],
                device_id={"sector": to}, device_id_type=MESH,
            )
            for side, to in ((0, prv), (1, nxt))
        ]

    def share_edges(field, ref):
        nb_send[0, field] = sector_rows(ref, 0)
        nb_send[1, field] = sector_rows(ref, LOCAL - 1)
        copies = neighbour_copies(field)
        for copy in copies:
            copy.start()
        return copies

    def send_all(src, dst, stage, ssem, rsem):
        def one(i, carry):
            to = lax.rem(me + i, ns)
            pltpu.make_async_remote_copy(
                src.at[to], dst.at[me], ssem.at[stage], rsem.at[stage],
                device_id={"sector": to}, device_id_type=MESH,
            ).start()
            return carry

        lax.fori_loop(1, ns, one, 0)
        dst[me] = src[me]

    def wait_all(src, dst, stage, ssem, rsem):
        most = pl.ds(0, ns - 1)
        return pltpu.make_async_remote_copy(
            src.at[most], dst.at[most], ssem.at[stage], rsem.at[stage],
            device_id={"sector": nxt}, device_id_type=MESH,
        )

    edge0 = share_edges(0, yp0)
    send_all(send1, rcv1, 0, a_ssem, a_rsem)
    edge1 = share_edges(1, yp1)

    for copy in int_copies:
        copy.wait()
    dof = lax.broadcasted_iota(jnp.int32, (DOF, 128), 0)
    mats_tri = jnp.where(
        jnp.abs(
            lax.broadcasted_iota(jnp.int32, (DOF, DOF), 0)
            - lax.broadcasted_iota(jnp.int32, (DOF, DOF), 1)
        )
        == 1,
        coupling,
        0.0,
    ).astype(BF16)
    diag = [None] * LOCAL
    for j in range(LOCAL + 1):
        left_ref, mask_ref, lrow = (cl_n, cm_n, LOCAL - 1) if j == 0 else (cl, cm, j - 1)
        right_ref, rrow = (cr_n, 0) if j == LOCAL else (cr, j)
        left = left_ref[pl.ds(lrow, 1), :]
        mask = mask_ref[pl.ds(lrow, 1), :]
        right = right_ref[pl.ds(rrow, 1), :]
        k = jnp.where(mask == 1, k_stick, jnp.where(mask == 2, k_slip, 0.0))
        at_left = jnp.where(dof == left, 1.0, 0.0).astype(BF16)
        at_right = jnp.where(dof == right, 1.0, 0.0).astype(BF16)
        k_left = jnp.where(dof == left, jnp.broadcast_to(k, (DOF, 128)), 0.0).astype(BF16)
        k8 = jnp.broadcast_to(k, (8, 128)).astype(BF16)
        if j > 0:
            mats[j - 1, 0:DOF, :] = dot(at_right, k_left, (1, 1)).astype(BF16)
            more = dot(k8, at_left, (1, 1))
            diag[j - 1] = more if diag[j - 1] is None else diag[j - 1] + more
        if j < LOCAL:
            mats[j, DOF:2 * DOF, :] = dot(k_left, at_right, (1, 1)).astype(BF16)
            mats[j, 2 * DOF:3 * DOF, :] = mats_tri
            diag[j] = dot(k8, at_right, (1, 1))
    row8 = lax.broadcasted_iota(jnp.int32, (8, 128), 0)
    total_k = stiff[...]
    for s in range(LOCAL):
        total_k = total_k + jnp.where(row8 == s, diag[s][:, 0:128], 0.0)
        total_k = total_k + jnp.where(row8 == LOCAL + s, diag[s][:, 128:256], 0.0)
    keff[...] = total_k

    def cross(own, next_first, prev_last, dst):
        chain = [prev_last] + own + [next_first]
        for s in range(LOCAL):
            lhs = jnp.concatenate([chain[s + 2], chain[s], chain[s + 1]], axis=1)
            out = dot(lhs, mats[s])
            dst[pl.ds(s, cols, stride=8), :] = out[:, 0:128]
            dst[pl.ds(4 + s, cols, stride=8), :] = out[:, 128:256]

    def cross_of(field, ref, dst):
        cross(
            [sector_rows(ref, s) for s in range(LOCAL)], nb_rcv[0, field], nb_rcv[1, field], dst
        )

    def times_k(rows_value):
        tiles = rows_value.reshape(rows_value.shape[0] // 8, 8, 128)
        return (tiles * keff[...][None]).reshape(rows_value.shape)

    for copy in edge0:
        copy.wait()
    cross_of(0, yp0, cross0)

    def second(i, carry):
        at = pl.ds(pl.multiple_of(i * block, block), block)
        y0 = yp0[at, :]
        w1 = w_acc[at, :] + cross0[at, :] - times_k(y0)
        v1 = H1 * w1 + e1[at, :]
        p2 = p_acc[at, :] + v1
        y2 = H2 * p2 + e2p[at, :]
        yp2[at, :] = y2
        p_acc[at, :] = p2
        w_acc[at, :] = w1 - damping * v1
        per = block // 16
        send2[pl.ds(i * per, per)] = low_of_pairs(C1 * y0 + C2 * yp1[at, :] + y2).astype(BF16)
        return carry

    lax.fori_loop(0, blocks, second, 0)
    send_all(send2, rcv2, 1, a_ssem, a_rsem)
    edge2 = share_edges(2, yp2)

    coef_load.wait()

    def loads_of(rhs, acc):
        width = rhs.shape[1] // AERO
        acc[...] = jnp.zeros_like(acc)

        def one(i, carry):
            pair = []
            tables = []
            for n in range(2):
                pick = jnp.where(smat[...] == (2 * i + n).astype(F32), 1.0, 0.0).astype(BF16)
                pair.append(dot(pick, rhs).astype(BF16))
                tables.append(coef[pl.ds(pl.multiple_of((2 * i + n) * AERO, AERO), AERO), :])
            lhs = jnp.concatenate(
                [
                    jnp.concatenate([g[:, c * AERO:(c + 1) * AERO] for g in pair], axis=1)
                    for c in range(width)
                ],
                axis=0,
            )
            acc[...] += dot(lhs, jnp.concatenate(tables, axis=1), (1, 1))
            return carry

        lax.fori_loop(0, TABLES // 2, one, 0)

    def by_sector(received):
        value = received.astype(F32).reshape(ns // 2, 2, 8, received.shape[2])
        first, second_ = swap_halves(value[:, 0], value[:, 1])
        return first.reshape(sectors, -1), second_.reshape(sectors, -1)

    def by_device(first, second_):
        lo, hi = swap_halves(
            first.reshape(ns // 2, 8, 128), second_.reshape(ns // 2, 8, 128)
        )
        return jnp.stack([lo, hi], axis=1).reshape(ns, 8, 128)

    wait_all(send1, rcv1, 0, a_ssem, a_rsem).wait()
    loads_of(jnp.concatenate(by_sector(rcv1[...]), axis=1).astype(BF16), acc1)
    a0 = [acc1[2 * c * sectors:(2 * c + 1) * sectors, :] for c in range(2)]
    b1 = [acc1[(2 * c + 1) * sectors:(2 * c + 2) * sectors, :] for c in range(2)]
    place = lax.broadcasted_iota(jnp.int32, (sectors, 128), 0) % LOCAL
    beside = [
        jnp.where(
            place == 0,
            pltpu.roll(a, 1, 0),
            jnp.where(place == LOCAL - 1, pltpu.roll(a, sectors - 1, 0), 0.0),
        )
        for a in a0
    ]
    send3[:, :, 0:128] = by_device(*a0).astype(BF16)
    send3[:, :, 128:256] = by_device(*beside).astype(BF16)
    send3[:, :, 256:384] = by_device(*b1).astype(BF16)
    send_all(send3, rcv3, 0, r_ssem, r_rsem)

    wait_all(send2, rcv2, 1, a_ssem, a_rsem).wait()
    rest = by_sector(rcv2[...])
    loads_of(
        jnp.concatenate(
            [rest[c] + HH * acc1[2 * c * sectors:(2 * c + 1) * sectors, :] for c in range(2)],
            axis=1,
        ).astype(BF16),
        acc2,
    )
    send4[...] = by_device(acc2[0:sectors, :], acc2[sectors:2 * sectors, :]).astype(BF16)
    send_all(send4, rcv4, 1, r_ssem, r_rsem)

    for copy in edge1 + edge2:
        copy.wait()
    cross_of(1, yp1, cross1)
    cross_of(2, yp2, cross2)

    def third(i, carry):
        at = pl.ds(pl.multiple_of(i * block, block), block)
        w2 = w_acc[at, :] + cross1[at, :] - times_k(yp1[at, :])
        v2 = H2 * w2 + e2w[at, :]
        p_acc[at, :] = p_acc[at, :] + v2
        w_acc[at, :] = w2 - damping * v2 + cross2[at, :] - times_k(yp2[at, :])
        return carry

    lax.fori_loop(0, blocks, third, 0)

    wait_all(send3, rcv3, 0, r_ssem, r_rsem).wait()

    def spread(i, carry):
        per = block // 16
        at = pl.ds(pl.multiple_of(i * block, block), block)
        got = rcv3[pl.ds(i * per, per)].astype(F32)
        a0r[at, :] = pairs_of_low(got[:, :, 0:128])
        halo[at, :] = pairs_of_low(got[:, :, 128:256])
        p3 = p_acc[at, :] + pairs_of_low(got[:, :, 256:384])
        st[0, at, :] = p3
        return carry + jnp.sum((p3 * p3).reshape(block // 8, 8, 128), axis=0)

    squares = lax.fori_loop(0, blocks, spread, jnp.zeros((8, 128), F32))
    out_p = pltpu.make_async_copy(st.at[0], out_hbm.at[0], out_sem.at[0])
    out_p.start()

    none = jnp.zeros((cols, 128), BF16)

    def surface_rows(ref, s):
        return jnp.concatenate([ref[pl.ds(s, cols, stride=8), :].astype(BF16), none], axis=1)

    cross(
        [surface_rows(a0r, s) for s in range(LOCAL)],
        surface_rows(halo, LOCAL - 1), surface_rows(halo, 0), cross0,
    )

    def fourth(i, carry):
        at = pl.ds(pl.multiple_of(i * block, block), block)
        w_acc[at, :] = w_acc[at, :] + HH * (cross0[at, :] - times_k(a0r[at, :]))
        return carry

    lax.fori_loop(0, blocks, fourth, 0)

    wait_all(send4, rcv4, 1, r_ssem, r_rsem).wait()

    def fifth(i, carry):
        per = block // 16
        at = pl.ds(pl.multiple_of(i * block, block), block)
        w3 = w_acc[at, :] + pairs_of_low(rcv4[pl.ds(i * per, per)].astype(F32))
        st[1, at, :] = w3
        return carry + jnp.sum((w3 * w3).reshape(block // 8, 8, 128), axis=0)

    squares = lax.fori_loop(0, blocks, fifth, squares)
    out_w = pltpu.make_async_copy(st.at[1], out_hbm.at[1], out_sem.at[1])
    out_w.start()

    part[...] = jnp.sum(squares, axis=0, keepdims=True)

    def to_col(i, carry):
        to = lax.rem(mycol + i, nc)
        pltpu.make_async_remote_copy(
            part, colsum.at[mycol], a_ssem.at[2], a_rsem.at[2],
            device_id={"col": to}, device_id_type=MESH,
        ).start()
        return carry

    lax.fori_loop(1, nc, to_col, 0)
    colsum[mycol] = part[...]
    most = pl.ds(0, nc - 1)
    pltpu.make_async_remote_copy(
        colsum.at[most], colsum.at[most], a_ssem.at[2], a_rsem.at[2],
        device_id={"sector": nxt}, device_id_type=MESH,
    ).wait()
    secpart[...] = jnp.sum(colsum[...], axis=0)

    def to_sector(i, carry):
        to = lax.rem(me + i, ns)
        pltpu.make_async_remote_copy(
            secpart, secsum.at[me], r_ssem.at[2], r_rsem.at[2],
            device_id={"sector": to}, device_id_type=MESH,
        ).start()
        return carry

    lax.fori_loop(1, ns, to_sector, 0)
    secsum[me] = secpart[...]
    wait_all(secsum, secsum, 2, r_ssem, r_rsem).wait()
    everything = jnp.sum(jnp.sum(secsum[...], axis=0), axis=1, keepdims=True)
    growth_ref[...] = jnp.broadcast_to(jnp.sqrt(everything / total_count + 1e-6), (1, 128))
    out_p.wait()
    out_w.wait()


def per_device(
    ns, nc, prev_nodes, stiffness, aero_coef, offset_slot, contact_left, contact_right, contact_mask
):
    cols = prev_nodes.shape[2]
    rows = cols * 8
    sectors = ns * LOCAL
    x = prev_nodes.reshape(8, cols, LOCAL, 2, 128).transpose(0, 1, 3, 2, 4).reshape(8, rows, 128)
    stiff = stiffness.reshape(LOCAL, 2, 128).transpose(1, 0, 2).reshape(8, 128)
    vm = pltpu.VMEM
    big = vm((rows, 128), F32)
    ints = vm((LOCAL, 128), jnp.int32)
    dma = pltpu.SemaphoreType.DMA
    any_spec = pl.BlockSpec(memory_space=pl.ANY)
    state, growth = pl.pallas_call(
        functools.partial(kernel, ns, nc, float(2 * cols * nc * sectors * DOF)),
        out_shape=(
            jax.ShapeDtypeStruct((2, rows, 128), F32),
            jax.ShapeDtypeStruct((1, 128), F32),
        ),
        in_specs=[any_spec] * 7,
        out_specs=(any_spec, pl.BlockSpec(memory_space=pltpu.VMEM)),
        scratch_shapes=[
            vm((8, rows, 128), F32),
            vm((8, 128), F32),
            vm((TABLES * AERO, AERO), BF16),
            vm((1, sectors), jnp.int32),
            ints, ints, ints, ints, ints, ints,
            vm((8, 128), F32),
            vm((LOCAL, 3 * DOF, DOF), BF16),
            vm((sectors, sectors), F32),
            big, big, big, big, big, big, big, big,
            big, big, big, big, big,
            vm((2, rows, 128), F32),
            vm((ns, 8, 256), BF16), vm((ns, 8, 256), BF16),
            vm((ns, 8, 128), BF16), vm((ns, 8, 128), BF16),
            vm((ns, 8, 384), BF16), vm((ns, 8, 384), BF16),
            vm((ns, 8, 128), BF16), vm((ns, 8, 128), BF16),
            vm((2, 3, cols, DOF), BF16), vm((2, 3, cols, DOF), BF16),
            vm((4 * sectors, AERO), F32),
            vm((2 * sectors, AERO), F32),
            vm((1, 128), F32),
            vm((nc, 1, 128), F32),
            vm((ns, 1, 128), F32),
            vm((1, 128), F32),
            dma((9,)), dma((5,)), dma((2,)),
            dma((3,)), dma((3,)), dma((2, 3)), dma((2, 3)),
            dma((3,)), dma((3,)), dma((3,)), dma((3,)),
        ],
        compiler_params=pltpu.CompilerParams(
            collective_id=0, has_side_effects=True, vmem_limit_bytes=60 << 20
        ),
        name="sweep",
    )(
        x, stiff, aero_coef.reshape(TABLES * AERO, AERO), offset_slot.reshape(1, sectors),
        contact_left, contact_right, contact_mask,
    )
    value = growth[0, 0]
    scaled = state / value
    scaled = scaled.reshape(2, cols, 2, LOCAL, 128).transpose(0, 1, 3, 2, 4)
    return scaled.reshape(2, cols, LOCAL, DOF), value


def solution(mesh):
    ns, nc = mesh.shape["sector"], mesh.shape["col"]
    placed = (
        P(None, None, "col", "sector", None),
        P("sector", None),
        P(),
        P(),
        P("sector", None),
        P("sector", None),
        P("sector", None),
    )
    return jax.shard_map(
        functools.partial(per_device, ns, nc),
        mesh=mesh,
        in_specs=placed,
        out_specs=(P(None, "col", "sector", None), P()),
        check_vma=False,
    )
```

profile of v0, /device:TPU:1, one launch (start us, length us, event | category | flops | bytes accessed | tf_op | source)
XLA Modules:
  0.0 52.2 jit_solution(5759496619205188067)
XLA Ops:
  0.6 47.5 %sweep.1 = (f32[2,512,128]{2,1,0:T(8,128)}, f32[1,128]{1,0:T(1,128)}) custom-call(f32[8,512,128]{2,1,0:T(8,128)} %bitcast.19, f32[8,128]{1,0:T(8,128)} %bitcast.22, bf16[4096,128]{1,0:T(8,128)(2,1)} %bitcast.20, s32[1,128]{1,0:T(1,128)} %bitcast.23, s32[4,128]{1,0:T(4,128)} %cl_hbm.1, s32[4,128]{1,0:T(4,128)} %cr_hbm.1, s32[4,128]{1,0:T(4,128)} %cm_hbm.1), custom_call_target="tpu_custom_call" | custom-call | tf_op jit(solution)/shard_map/sweep/pallas_call | solution.py:494
  48.1 2.4 %broadcast_divide_fusion = f32[2,512,128]{2,1,0:T(8,128)} fusion(f32[2,512,128]{2,1,0:T(8,128)} %get-tuple-element.4, f32[]{:T(128)} %bitcast.24), kind=kLoop, calls=%fused_computation | loop fusion | flops 131072 | bytes 1048580 | tf_op jit(solution)/shard_map/div | solution.py:538
where the time goes:
time: 52.4 us; the launch traced here: 52.2 us
  Pallas kernels  47.5 us (91%)
  other arithmetic  2.44 us (5%)
  between operations  2.34 us (4%)
    pallas_call x1, Pallas kernels, per_device(): pl.pallas_call(functools.partial(kernel, ns, nc, float(2 * cols * nc * se...  47.5 us
    div x1, other arithmetic, per_device(): scaled = state / value  2.44 us

commit v1 on v0

--- a/solution.py
+++ b/solution.py
@@ -91,7 +91,7 @@
     x_hbm, stiff_hbm, coef_hbm, slot_hbm, cl_hbm, cr_hbm, cm_hbm,
     out_hbm, growth_ref,
     xs, stiff, coef, slot, cl, cr, cm, cl_n, cr_n, cm_n,
-    keff, mats, smat,
+    keff, mats, picks, tabled,
     yp0, yp1, yp2, a0r, halo, cross0, cross1, cross2,
     w_acc, p_acc, e1, e2p, e2w, st,
     send1, rcv1, send2, rcv2, send3, rcv3, send4, rcv4,
@@ -123,6 +123,9 @@
         )
         return carry
 
+    loads = [pltpu.make_async_copy(x_hbm.at[n], xs.at[n], load_sem.at[n]) for n in range(8)]
+    for copy in loads:
+        copy.start()
     smalls = [
         pltpu.make_async_copy(src, dst, small_sem.at[n])
         for n, (src, dst) in enumerate(
@@ -131,32 +134,12 @@
     ]
     for copy in smalls:
         copy.start()
-    loads = [pltpu.make_async_copy(x_hbm.at[n], xs.at[n], load_sem.at[n]) for n in range(8)]
-    for copy in loads:
-        copy.start()
+    for to in (prv, nxt):
+        pl.semaphore_signal(barrier, inc=1, device_id={"sector": to}, device_id_type=MESH)
+    lax.fori_loop(2, ns - 1, greet_sector, 0)
+    lax.fori_loop(1, nc, greet_col, 0)
     coef_load = pltpu.make_async_copy(coef_hbm, coef, load_sem.at[8])
     coef_load.start()
-    lax.fori_loop(1, ns, greet_sector, 0)
-    lax.fori_loop(1, nc, greet_col, 0)
-    for copy in smalls:
-        copy.wait()
-
-    smat[...] = pltpu.roll(
-        jnp.broadcast_to(slot[...].astype(F32), (sectors, sectors)), 0, 1, stride=1, stride_axis=0
-    )
-
-    pl.semaphore_wait(barrier, ns + nc - 2)
-
-    int_copies = [
-        pltpu.make_async_remote_copy(
-            src, dst, int_ssem.at[n], int_rsem.at[n],
-            device_id={"sector": to}, device_id_type=MESH,
-        )
-        for n, (src, dst, to) in enumerate([(cl, cl_n, nxt), (cm, cm_n, nxt), (cr, cr_n, prv)])
-    ]
-    for copy in int_copies:
-        copy.start()
-
     for copy in loads:
         copy.wait()
 
@@ -194,7 +177,7 @@
     def sector_rows(ref, s):
         return jnp.concatenate(
             [ref[pl.ds(s, cols, stride=8), :], ref[pl.ds(4 + s, cols, stride=8), :]], axis=1
-        ).astype(BF16)
+        )
 
     def neighbour_copies(field):
         return [
@@ -206,13 +189,9 @@
             for side, to in ((0, prv), (1, nxt))
         ]
 
-    def share_edges(field, ref):
-        nb_send[0, field] = sector_rows(ref, 0)
-        nb_send[1, field] = sector_rows(ref, LOCAL - 1)
-        copies = neighbour_copies(field)
-        for copy in copies:
-            copy.start()
-        return copies
+    def fill_edges(field, ref):
+        nb_send[0, field] = sector_rows(ref, 0).astype(BF16)
+        nb_send[1, field] = sector_rows(ref, LOCAL - 1).astype(BF16)
 
     def send_all(src, dst, stage, ssem, rsem):
         def one(i, carry):
@@ -233,9 +212,32 @@
             device_id={"sector": nxt}, device_id_type=MESH,
         )
 
-    edge0 = share_edges(0, yp0)
+    fill_edges(0, yp0)
+    for copy in smalls:
+        copy.wait()
+    int_copies = [
+        pltpu.make_async_remote_copy(
+            src, dst, int_ssem.at[n], int_rsem.at[n],
+            device_id={"sector": to}, device_id_type=MESH,
+        )
+        for n, (src, dst, to) in enumerate([(cl, cl_n, nxt), (cm, cm_n, nxt), (cr, cr_n, prv)])
+    ]
+    edge0, edge1, edge2 = [neighbour_copies(field) for field in range(3)]
+
+    pl.semaphore_wait(barrier, ns + nc - 2)
+
+    for copy in int_copies + edge0:
+        copy.start()
     send_all(send1, rcv1, 0, a_ssem, a_rsem)
-    edge1 = share_edges(1, yp1)
+    fill_edges(1, yp1)
+    for copy in edge1:
+        copy.start()
+
+    smat = pltpu.roll(
+        jnp.broadcast_to(slot[...].astype(F32), (sectors, sectors)), 0, 1, stride=1, stride_axis=0
+    )
+    for k in range(TABLES):
+        picks[:, k * sectors:(k + 1) * sectors] = jnp.where(smat == float(k), 1.0, 0.0).astype(BF16)
 
     for copy in int_copies:
         copy.wait()
@@ -286,8 +288,23 @@
 
     def cross_of(field, ref, dst):
         cross(
-            [sector_rows(ref, s) for s in range(LOCAL)], nb_rcv[0, field], nb_rcv[1, field], dst
-        )
+            [sector_rows(ref, s).astype(BF16) for s in range(LOCAL)],
+            nb_rcv[0, field], nb_rcv[1, field], dst,
+        )
+
+    def fine_cross_of(field, ref, dst):
+        none = jnp.zeros((cols, DOF), BF16)
+        chain = [jnp.concatenate([nb_rcv[1, field], none], axis=0)]
+        for s in range(LOCAL):
+            value = sector_rows(ref, s)
+            high = value.astype(BF16)
+            chain.append(jnp.concatenate([high, (value - high.astype(F32)).astype(BF16)], axis=0))
+        chain.append(jnp.concatenate([nb_rcv[0, field], none], axis=0))
+        for s in range(LOCAL):
+            both = dot(jnp.concatenate([chain[s + 2], chain[s], chain[s + 1]], axis=1), mats[s])
+            out = both[0:cols] + both[cols:2 * cols]
+            dst[pl.ds(s, cols, stride=8), :] = out[:, 0:128]
+            dst[pl.ds(4 + s, cols, stride=8), :] = out[:, 128:256]
 
     def times_k(rows_value):
         tiles = rows_value.reshape(rows_value.shape[0] // 8, 8, 128)
@@ -313,32 +330,23 @@
 
     lax.fori_loop(0, blocks, second, 0)
     send_all(send2, rcv2, 1, a_ssem, a_rsem)
-    edge2 = share_edges(2, yp2)
+    fill_edges(2, yp2)
+    for copy in edge2:
+        copy.start()
 
     coef_load.wait()
 
-    def loads_of(rhs, acc):
-        width = rhs.shape[1] // AERO
-        acc[...] = jnp.zeros_like(acc)
-
-        def one(i, carry):
-            pair = []
-            tables = []
+    def loads_of(surfaces, acc):
+        parts = len(surfaces)
+        lhs = jnp.concatenate(surfaces, axis=0).astype(BF16)
+        for k in range(0, TABLES, 2):
+            u = dot(lhs, coef[k * AERO:(k + 2) * AERO, :], (1, 1)).astype(BF16)
             for n in range(2):
-                pick = jnp.where(smat[...] == (2 * i + n).astype(F32), 1.0, 0.0).astype(BF16)
-                pair.append(dot(pick, rhs).astype(BF16))
-                tables.append(coef[pl.ds(pl.multiple_of((2 * i + n) * AERO, AERO), AERO), :])
-            lhs = jnp.concatenate(
-                [
-                    jnp.concatenate([g[:, c * AERO:(c + 1) * AERO] for g in pair], axis=1)
-                    for c in range(width)
-                ],
-                axis=0,
-            )
-            acc[...] += dot(lhs, jnp.concatenate(tables, axis=1), (1, 1))
-            return carry
-
-        lax.fori_loop(0, TABLES // 2, one, 0)
+                for c in range(parts):
+                    tabled[
+                        (k + n) * sectors:(k + n + 1) * sectors, c * AERO:(c + 1) * AERO
+                    ] = u[c * sectors:(c + 1) * sectors, n * AERO:(n + 1) * AERO]
+        acc[...] = dot(picks[...], tabled[:, 0:parts * AERO])
 
     def by_sector(received):
         value = received.astype(F32).reshape(ns // 2, 2, 8, received.shape[2])
@@ -352,9 +360,10 @@
         return jnp.stack([lo, hi], axis=1).reshape(ns, 8, 128)
 
     wait_all(send1, rcv1, 0, a_ssem, a_rsem).wait()
-    loads_of(jnp.concatenate(by_sector(rcv1[...]), axis=1).astype(BF16), acc1)
-    a0 = [acc1[2 * c * sectors:(2 * c + 1) * sectors, :] for c in range(2)]
-    b1 = [acc1[(2 * c + 1) * sectors:(2 * c + 2) * sectors, :] for c in range(2)]
+    arrived = by_sector(rcv1[...])
+    loads_of([arrived[c][:, f * AERO:(f + 1) * AERO] for c in range(2) for f in range(2)], acc1)
+    a0 = [acc1[:, 2 * c * AERO:(2 * c + 1) * AERO] for c in range(2)]
+    b1 = [acc1[:, (2 * c + 1) * AERO:(2 * c + 2) * AERO] for c in range(2)]
     place = lax.broadcasted_iota(jnp.int32, (sectors, 128), 0) % LOCAL
     beside = [
         jnp.where(
@@ -369,22 +378,10 @@
     send3[:, :, 256:384] = by_device(*b1).astype(BF16)
     send_all(send3, rcv3, 0, r_ssem, r_rsem)
 
-    wait_all(send2, rcv2, 1, a_ssem, a_rsem).wait()
-    rest = by_sector(rcv2[...])
-    loads_of(
-        jnp.concatenate(
-            [rest[c] + HH * acc1[2 * c * sectors:(2 * c + 1) * sectors, :] for c in range(2)],
-            axis=1,
-        ).astype(BF16),
-        acc2,
-    )
-    send4[...] = by_device(acc2[0:sectors, :], acc2[sectors:2 * sectors, :]).astype(BF16)
-    send_all(send4, rcv4, 1, r_ssem, r_rsem)
-
     for copy in edge1 + edge2:
         copy.wait()
-    cross_of(1, yp1, cross1)
-    cross_of(2, yp2, cross2)
+    fine_cross_of(1, yp1, cross1)
+    fine_cross_of(2, yp2, cross2)
 
     def third(i, carry):
         at = pl.ds(pl.multiple_of(i * block, block), block)
@@ -395,6 +392,14 @@
         return carry
 
     lax.fori_loop(0, blocks, third, 0)
+
+    wait_all(send2, rcv2, 1, a_ssem, a_rsem).wait()
+    rest = by_sector(rcv2[...])
+    loads_of(
+        [rest[c] + HH * acc1[:, 2 * c * AERO:(2 * c + 1) * AERO] for c in range(2)], acc2
+    )
+    send4[...] = by_device(acc2[:, 0:AERO], acc2[:, AERO:2 * AERO])
+    send_all(send4, rcv4, 1, r_ssem, r_rsem)
 
     wait_all(send3, rcv3, 0, r_ssem, r_rsem).wait()
 
@@ -434,7 +439,7 @@
     def fifth(i, carry):
         per = block // 16
         at = pl.ds(pl.multiple_of(i * block, block), block)
-        w3 = w_acc[at, :] + pairs_of_low(rcv4[pl.ds(i * per, per)].astype(F32))
+        w3 = w_acc[at, :] + pairs_of_low(rcv4[pl.ds(i * per, per)])
         st[1, at, :] = w3
         return carry + jnp.sum((w3 * w3).reshape(block // 8, 8, 128), axis=0)
 
@@ -507,17 +512,18 @@
             ints, ints, ints, ints, ints, ints,
             vm((8, 128), F32),
             vm((LOCAL, 3 * DOF, DOF), BF16),
-            vm((sectors, sectors), F32),
+            vm((sectors, TABLES * sectors), BF16),
+            vm((TABLES * sectors, 4 * AERO), BF16),
             big, big, big, big, big, big, big, big,
             big, big, big, big, big,
             vm((2, rows, 128), F32),
             vm((ns, 8, 256), BF16), vm((ns, 8, 256), BF16),
             vm((ns, 8, 128), BF16), vm((ns, 8, 128), BF16),
             vm((ns, 8, 384), BF16), vm((ns, 8, 384), BF16),
-            vm((ns, 8, 128), BF16), vm((ns, 8, 128), BF16),
+            vm((ns, 8, 128), F32), vm((ns, 8, 128), F32),
             vm((2, 3, cols, DOF), BF16), vm((2, 3, cols, DOF), BF16),
-            vm((4 * sectors, AERO), F32),
-            vm((2 * sectors, AERO), F32),
+            vm((sectors, 4 * AERO), F32),
+            vm((sectors, 2 * AERO), F32),
             vm((1, 128), F32),
             vm((nc, 1, 128), F32),
             vm((ns, 1, 128), F32),

time: 52.4 us -> 47.7 us (0.910)
  Pallas kernels: 47.5 us -> 42.8 us
    pallas_call x1, Pallas kernels: 47.5 us -> 42.8 us  [per_device(): pl.pallas_call(functools.partial(kernel, ns, nc, float(2 * cols * nc * se...]
where the time goes in v1:
time: 47.7 us; the launch traced here: 47.6 us
  Pallas kernels  42.8 us (90%)
  other arithmetic  2.44 us (5%)
  between operations  2.34 us (5%)
    pallas_call x1, Pallas kernels, per_device(): pl.pallas_call(functools.partial(kernel, ns, nc, float(2 * cols * nc * se...  42.8 us
    div x1, other arithmetic, per_device(): scaled = state / value  2.44 us

profile of v1, /device:TPU:1, one launch (start us, length us, event | category | flops | bytes accessed | tf_op | source)
XLA Modules:
  0.0 47.6 jit_solution(7290921140714332680)
XLA Ops:
  0.6 42.8 %sweep.1 = (f32[2,512,128]{2,1,0:T(8,128)}, f32[1,128]{1,0:T(1,128)}) custom-call(f32[8,512,128]{2,1,0:T(8,128)} %bitcast.19, f32[8,128]{1,0:T(8,128)} %bitcast.22, bf16[4096,128]{1,0:T(8,128)(2,1)} %bitcast.20, s32[1,128]{1,0:T(1,128)} %bitcast.23, s32[4,128]{1,0:T(4,128)} %cl_hbm.1, s32[4,128]{1,0:T(4,128)} %cr_hbm.1, s32[4,128]{1,0:T(4,128)} %cm_hbm.1), custom_call_target="tpu_custom_call" | custom-call | tf_op jit(solution)/shard_map/sweep/pallas_call | solution.py:499
  43.4 2.4 %broadcast_divide_fusion = f32[2,512,128]{2,1,0:T(8,128)} fusion(f32[2,512,128]{2,1,0:T(8,128)} %get-tuple-element.4, f32[]{:T(128)} %bitcast.24), kind=kLoop, calls=%fused_computation | loop fusion | flops 131072 | bytes 1048580 | tf_op jit(solution)/shard_map/div | solution.py:544

commit v2 on v1

--- a/solution.py
+++ b/solution.py
@@ -89,22 +89,23 @@
 def kernel(
     ns, nc, total_count,
     x_hbm, stiff_hbm, coef_hbm, slot_hbm, cl_hbm, cr_hbm, cm_hbm,
-    out_hbm, growth_ref,
+    st, growth_ref,
     xs, stiff, coef, slot, cl, cr, cm, cl_n, cr_n, cm_n,
     keff, mats, picks, tabled,
-    yp0, yp1, yp2, a0r, halo, cross0, cross1, cross2,
-    w_acc, p_acc, e1, e2p, e2w, st,
-    send1, rcv1, send2, rcv2, send3, rcv3, send4, rcv4,
-    nb_send, nb_rcv, acc1, acc2, part, colsum, secsum, secpart,
-    load_sem, small_sem, out_sem,
+    yp0, yp1, yp2, a0r, cross0, cross1, cross2,
+    w_acc, p_acc, e1, e2p, e2w,
+    send1, rcv1, send2, rcv2, send3, rcv3, send4, rcv4, send5, rcv5,
+    nb_send, nb_rcv, nb_low, nb_low_rcv, acc1, acc2, part, colsum, secsum, secpart,
+    load_sem, small_sem,
     int_ssem, int_rsem, nb_ssem, nb_rsem, a_ssem, a_rsem, r_ssem, r_rsem,
+    low_ssem, low_rsem,
 ):
     me = lax.axis_index("sector")
     mycol = lax.axis_index("col")
     rows = xs.shape[1]
     cols = 2 * ns
     sectors = LOCAL * ns
-    block = min(64, rows)
+    block = min(64, rows // 4)
     blocks = rows // block
     nxt = lax.rem(me + 1, ns)
     prv = lax.rem(me + ns - 1, ns)
@@ -117,13 +118,29 @@
         )
         return carry
 
+    def greet_other(i, carry):
+        pl.semaphore_signal(
+            barrier, inc=1,
+            device_id={"sector": lax.rem(me + ns // 2, ns), "col": lax.rem(mycol + i, nc)},
+            device_id_type=MESH,
+        )
+        return carry
+
     def greet_col(i, carry):
         pl.semaphore_signal(
             barrier, inc=1, device_id={"col": lax.rem(mycol + i, nc)}, device_id_type=MESH
         )
         return carry
 
-    loads = [pltpu.make_async_copy(x_hbm.at[n], xs.at[n], load_sem.at[n]) for n in range(8)]
+    quarter = rows // 4
+    loads = [
+        pltpu.make_async_copy(
+            x_hbm.at[:, pl.ds(n * quarter, quarter), :],
+            xs.at[:, pl.ds(n * quarter, quarter), :],
+            load_sem.at[n],
+        )
+        for n in range(4)
+    ]
     for copy in loads:
         copy.start()
     smalls = [
@@ -138,11 +155,9 @@
         pl.semaphore_signal(barrier, inc=1, device_id={"sector": to}, device_id_type=MESH)
     lax.fori_loop(2, ns - 1, greet_sector, 0)
     lax.fori_loop(1, nc, greet_col, 0)
-    coef_load = pltpu.make_async_copy(coef_hbm, coef, load_sem.at[8])
+    lax.fori_loop(1, nc, greet_other, 0)
+    coef_load = pltpu.make_async_copy(coef_hbm, coef, load_sem.at[4])
     coef_load.start()
-    for copy in loads:
-        copy.wait()
-
     def combine(i, carry):
         at = pl.ds(pl.multiple_of(i * block, block), block)
         p = [xs[2 * j, at, :] for j in range(4)]
@@ -172,7 +187,9 @@
         send1[pl.ds(i * per, per)] = chunk
         return carry
 
-    lax.fori_loop(0, blocks, combine, 0)
+    for n in range(4):
+        loads[n].wait()
+        lax.fori_loop(n * blocks // 4, (n + 1) * blocks // 4, combine, 0)
 
     def sector_rows(ref, s):
         return jnp.concatenate(
@@ -224,7 +241,7 @@
     ]
     edge0, edge1, edge2 = [neighbour_copies(field) for field in range(3)]
 
-    pl.semaphore_wait(barrier, ns + nc - 2)
+    pl.semaphore_wait(barrier, ns + 2 * nc - 3)
 
     for copy in int_copies + edge0:
         copy.start()
@@ -361,22 +378,12 @@
 
     wait_all(send1, rcv1, 0, a_ssem, a_rsem).wait()
     arrived = by_sector(rcv1[...])
-    loads_of([arrived[c][:, f * AERO:(f + 1) * AERO] for c in range(2) for f in range(2)], acc1)
-    a0 = [acc1[:, 2 * c * AERO:(2 * c + 1) * AERO] for c in range(2)]
-    b1 = [acc1[:, (2 * c + 1) * AERO:(2 * c + 2) * AERO] for c in range(2)]
-    place = lax.broadcasted_iota(jnp.int32, (sectors, 128), 0) % LOCAL
-    beside = [
-        jnp.where(
-            place == 0,
-            pltpu.roll(a, 1, 0),
-            jnp.where(place == LOCAL - 1, pltpu.roll(a, sectors - 1, 0), 0.0),
-        )
-        for a in a0
-    ]
-    send3[:, :, 0:128] = by_device(*a0).astype(BF16)
-    send3[:, :, 128:256] = by_device(*beside).astype(BF16)
-    send3[:, :, 256:384] = by_device(*b1).astype(BF16)
+    loads_of([arrived[c][:, 0:AERO] for c in range(2)], acc1)
+    send3[...] = by_device(acc1[:, 0:AERO], acc1[:, AERO:2 * AERO]).astype(BF16)
     send_all(send3, rcv3, 0, r_ssem, r_rsem)
+    loads_of([arrived[c][:, AERO:2 * AERO] for c in range(2)], acc2)
+    send5[...] = by_device(acc2[:, 0:AERO], acc2[:, AERO:2 * AERO]).astype(BF16)
+    send_all(send5, rcv5, 3, r_ssem, r_rsem)
 
     for copy in edge1 + edge2:
         copy.wait()
@@ -396,9 +403,9 @@
     wait_all(send2, rcv2, 1, a_ssem, a_rsem).wait()
     rest = by_sector(rcv2[...])
     loads_of(
-        [rest[c] + HH * acc1[:, 2 * c * AERO:(2 * c + 1) * AERO] for c in range(2)], acc2
-    )
-    send4[...] = by_device(acc2[:, 0:AERO], acc2[:, AERO:2 * AERO])
+        [rest[c] + HH * acc1[:, c * AERO:(c + 1) * AERO] for c in range(2)], acc2
+    )
+    send4[...] = by_device(acc2[:, 0:AERO], acc2[:, AERO:2 * AERO]).astype(BF16)
     send_all(send4, rcv4, 1, r_ssem, r_rsem)
 
     wait_all(send3, rcv3, 0, r_ssem, r_rsem).wait()
@@ -406,25 +413,43 @@
     def spread(i, carry):
         per = block // 16
         at = pl.ds(pl.multiple_of(i * block, block), block)
-        got = rcv3[pl.ds(i * per, per)].astype(F32)
-        a0r[at, :] = pairs_of_low(got[:, :, 0:128])
-        halo[at, :] = pairs_of_low(got[:, :, 128:256])
-        p3 = p_acc[at, :] + pairs_of_low(got[:, :, 256:384])
+        a0r[at, :] = pairs_of_low(rcv3[pl.ds(i * per, per)].astype(F32))
+        return carry
+
+    lax.fori_loop(0, blocks, spread, 0)
+
+    none = jnp.zeros((cols, 128), BF16)
+    own = [a0r[pl.ds(s, cols, stride=8), :].astype(BF16) for s in range(LOCAL)]
+    nb_low[0] = own[0]
+    nb_low[1] = own[LOCAL - 1]
+    edge_low = [
+        pltpu.make_async_remote_copy(
+            nb_low.at[side], nb_low_rcv.at[side], low_ssem.at[side], low_rsem.at[side],
+            device_id={"sector": to}, device_id_type=MESH,
+        )
+        for side, to in ((0, prv), (1, nxt))
+    ]
+    for copy in edge_low:
+        copy.start()
+
+    wait_all(send5, rcv5, 3, r_ssem, r_rsem).wait()
+
+    def close_p(i, carry):
+        per = block // 16
+        at = pl.ds(pl.multiple_of(i * block, block), block)
+        p3 = p_acc[at, :] + pairs_of_low(rcv5[pl.ds(i * per, per)].astype(F32))
         st[0, at, :] = p3
         return carry + jnp.sum((p3 * p3).reshape(block // 8, 8, 128), axis=0)
 
-    squares = lax.fori_loop(0, blocks, spread, jnp.zeros((8, 128), F32))
-    out_p = pltpu.make_async_copy(st.at[0], out_hbm.at[0], out_sem.at[0])
-    out_p.start()
-
-    none = jnp.zeros((cols, 128), BF16)
-
-    def surface_rows(ref, s):
-        return jnp.concatenate([ref[pl.ds(s, cols, stride=8), :].astype(BF16), none], axis=1)
-
+    squares = lax.fori_loop(0, blocks, close_p, jnp.zeros((8, 128), F32))
+
+    for copy in edge_low:
+        copy.wait()
     cross(
-        [surface_rows(a0r, s) for s in range(LOCAL)],
-        surface_rows(halo, LOCAL - 1), surface_rows(halo, 0), cross0,
+        [jnp.concatenate([v, none], axis=1) for v in own],
+        jnp.concatenate([nb_low_rcv[0], none], axis=1),
+        jnp.concatenate([nb_low_rcv[1], none], axis=1),
+        cross0,
     )
 
     def fourth(i, carry):
@@ -439,48 +464,53 @@
     def fifth(i, carry):
         per = block // 16
         at = pl.ds(pl.multiple_of(i * block, block), block)
-        w3 = w_acc[at, :] + pairs_of_low(rcv4[pl.ds(i * per, per)])
+        w3 = w_acc[at, :] + pairs_of_low(rcv4[pl.ds(i * per, per)].astype(F32))
         st[1, at, :] = w3
         return carry + jnp.sum((w3 * w3).reshape(block // 8, 8, 128), axis=0)
 
     squares = lax.fori_loop(0, blocks, fifth, squares)
-    out_w = pltpu.make_async_copy(st.at[1], out_hbm.at[1], out_sem.at[1])
-    out_w.start()
 
     part[...] = jnp.sum(squares, axis=0, keepdims=True)
 
-    def to_col(i, carry):
-        to = lax.rem(mycol + i, nc)
+    half = ns // 2
+    low, high = lax.rem(me, half), me // half
+    spot = high * nc + mycol
+
+    def over_high(i, carry):
+        to = lax.rem(spot + i, 2 * nc)
         pltpu.make_async_remote_copy(
-            part, colsum.at[mycol], a_ssem.at[2], a_rsem.at[2],
-            device_id={"col": to}, device_id_type=MESH,
+            part, colsum.at[spot], a_ssem.at[2], a_rsem.at[2],
+            device_id={"sector": low + half * (to // nc), "col": lax.rem(to, nc)},
+            device_id_type=MESH,
         ).start()
         return carry
 
-    lax.fori_loop(1, nc, to_col, 0)
-    colsum[mycol] = part[...]
-    most = pl.ds(0, nc - 1)
+    lax.fori_loop(1, 2 * nc, over_high, 0)
+    colsum[spot] = part[...]
+    most = pl.ds(0, 2 * nc - 1)
     pltpu.make_async_remote_copy(
         colsum.at[most], colsum.at[most], a_ssem.at[2], a_rsem.at[2],
         device_id={"sector": nxt}, device_id_type=MESH,
     ).wait()
     secpart[...] = jnp.sum(colsum[...], axis=0)
 
-    def to_sector(i, carry):
-        to = lax.rem(me + i, ns)
+    def over_low(i, carry):
+        to = lax.rem(low + i, half)
         pltpu.make_async_remote_copy(
-            secpart, secsum.at[me], r_ssem.at[2], r_rsem.at[2],
-            device_id={"sector": to}, device_id_type=MESH,
+            secpart, secsum.at[low], r_ssem.at[2], r_rsem.at[2],
+            device_id={"sector": high * half + to}, device_id_type=MESH,
         ).start()
         return carry
 
-    lax.fori_loop(1, ns, to_sector, 0)
-    secsum[me] = secpart[...]
-    wait_all(secsum, secsum, 2, r_ssem, r_rsem).wait()
+    lax.fori_loop(1, half, over_low, 0)
+    secsum[low] = secpart[...]
+    most_low = pl.ds(0, half - 1)
+    pltpu.make_async_remote_copy(
+        secsum.at[most_low], secsum.at[most_low], r_ssem.at[2], r_rsem.at[2],
+        device_id={"sector": nxt}, device_id_type=MESH,
+    ).wait()
     everything = jnp.sum(jnp.sum(secsum[...], axis=0), axis=1, keepdims=True)
     growth_ref[...] = jnp.broadcast_to(jnp.sqrt(everything / total_count + 1e-6), (1, 128))
-    out_p.wait()
-    out_w.wait()
 
 
 def per_device(
@@ -499,11 +529,11 @@
     state, growth = pl.pallas_call(
         functools.partial(kernel, ns, nc, float(2 * cols * nc * sectors * DOF)),
         out_shape=(
-            jax.ShapeDtypeStruct((2, rows, 128), F32),
-            jax.ShapeDtypeStruct((1, 128), F32),
+            pltpu.VMEM((2, rows, 128), F32),
+            pltpu.VMEM((1, 128), F32),
         ),
         in_specs=[any_spec] * 7,
-        out_specs=(any_spec, pl.BlockSpec(memory_space=pltpu.VMEM)),
+        out_specs=(pl.BlockSpec(memory_space=pltpu.VMEM), pl.BlockSpec(memory_space=pltpu.VMEM)),
         scratch_shapes=[
             vm((8, rows, 128), F32),
             vm((8, 128), F32),
@@ -513,24 +543,26 @@
             vm((8, 128), F32),
             vm((LOCAL, 3 * DOF, DOF), BF16),
             vm((sectors, TABLES * sectors), BF16),
-            vm((TABLES * sectors, 4 * AERO), BF16),
-            big, big, big, big, big, big, big, big,
+            vm((TABLES * sectors, 2 * AERO), BF16),
+            big, big, big, big, big, big, big,
             big, big, big, big, big,
-            vm((2, rows, 128), F32),
             vm((ns, 8, 256), BF16), vm((ns, 8, 256), BF16),
             vm((ns, 8, 128), BF16), vm((ns, 8, 128), BF16),
-            vm((ns, 8, 384), BF16), vm((ns, 8, 384), BF16),
-            vm((ns, 8, 128), F32), vm((ns, 8, 128), F32),
+            vm((ns, 8, 128), BF16), vm((ns, 8, 128), BF16),
+            vm((ns, 8, 128), BF16), vm((ns, 8, 128), BF16),
+            vm((ns, 8, 128), BF16), vm((ns, 8, 128), BF16),
             vm((2, 3, cols, DOF), BF16), vm((2, 3, cols, DOF), BF16),
-            vm((sectors, 4 * AERO), F32),
+            vm((2, cols, 128), BF16), vm((2, cols, 128), BF16),
+            vm((sectors, 2 * AERO), F32),
             vm((sectors, 2 * AERO), F32),
             vm((1, 128), F32),
-            vm((nc, 1, 128), F32),
-            vm((ns, 1, 128), F32),
+            vm((2 * nc, 1, 128), F32),
+            vm((ns // 2, 1, 128), F32),
             vm((1, 128), F32),
-            dma((9,)), dma((5,)), dma((2,)),
+            dma((5,)), dma((5,)),
             dma((3,)), dma((3,)), dma((2, 3)), dma((2, 3)),
-            dma((3,)), dma((3,)), dma((3,)), dma((3,)),
+            dma((3,)), dma((3,)), dma((4,)), dma((4,)),
+            dma((2,)), dma((2,)),
         ],
         compiler_params=pltpu.CompilerParams(
             collective_id=0, has_side_effects=True, vmem_limit_bytes=60 << 20

time: 47.7 us -> 43.8 us (0.918)
  Pallas kernels: 42.8 us -> 41 us
  other arithmetic: 2.44 us -> 0.87 us
  between operations: 2.34 us -> 1.81 us
    pallas_call x1, Pallas kernels: 42.8 us -> 41 us  [per_device(): pl.pallas_call(functools.partial(kernel, ns, nc, float(2 * cols * nc * se...]
    div x1, other arithmetic: 2.44 us -> 0.87 us  [per_device(): scaled = state / value]
where the time goes in v2:
time: 43.8 us; the launch traced here: 43.7 us
  Pallas kernels  41 us (94%)
  between operations  1.81 us (4%)
  other arithmetic  0.87 us (2%)
    pallas_call x1, Pallas kernels, per_device(): pl.pallas_call(functools.partial(kernel, ns, nc, float(2 * cols * nc * se...  41 us

profile of v2, /device:TPU:1, one launch (start us, length us, event | category | flops | bytes accessed | tf_op | source)
XLA Modules:
  0.0 43.7 jit_solution(13630185578861679221)
XLA Ops:
  0.6 41.0 %sweep.1 = (f32[2,512,128]{2,1,0:T(8,128)S(1)}, f32[1,128]{1,0:T(1,128)S(1)}) custom-call(f32[8,512,128]{2,1,0:T(8,128)} %bitcast.21, f32[8,128]{1,0:T(8,128)} %bitcast.24, bf16[4096,128]{1,0:T(8,128)(2,1)} %bitcast.22, s32[1,128]{1,0:T(1,128)} %bitcast.25, s32[4,128]{1,0:T(4,128)} %cl_hbm.1, s32[4,128]{1,0:T(4,128)} %cr_hbm.1, s32[4,128]{1,0:T(4,128)} %cm_hbm.1), custom_call_target="tpu_custom_call" | custom-call | tf_op jit(solution)/shard_map/sweep/pallas_call | solution.py:529
  41.6 0.9 %broadcast_divide_fusion = f32[2,512,128]{2,1,0:T(8,128)} fusion(f32[2,512,128]{2,1,0:T(8,128)S(1)} %get-tuple-element.4, f32[]{:T(128)S(1)} %bitcast.19), kind=kLoop, calls=%fused_computation | loop fusion | flops 131072 | bytes 1048580 | tf_op jit(solution)/shard_map/div | solution.py:576

commit v3 on v2

--- a/solution.py
+++ b/solution.py
@@ -80,6 +80,10 @@
     return jnp.stack([first, second], axis=1).reshape(chunks.shape[0] * 16, 128)
 
 
+def far_first(step, length):
+    return lax.rem(length // 2 + length + (1 - 2 * lax.rem(step, 2)) * ((step + 1) // 2), length)
+
+
 def dot(a, b, dims=(1, 0)):
     return lax.dot_general(
         a, b, (((dims[0],), (dims[1],)), ((), ())), preferred_element_type=F32
@@ -90,14 +94,14 @@
     ns, nc, total_count,
     x_hbm, stiff_hbm, coef_hbm, slot_hbm, cl_hbm, cr_hbm, cm_hbm,
     st, growth_ref,
-    xs, stiff, coef, slot, cl, cr, cm, cl_n, cr_n, cm_n,
-    keff, mats, picks, tabled,
+    xs, stiff, coef, slot, cl, cr, cm,
+    keff, mats, ends, picks, tabled,
     yp0, yp1, yp2, a0r, cross0, cross1, cross2,
     w_acc, p_acc, e1, e2p, e2w,
     send1, rcv1, send2, rcv2, send3, rcv3, send4, rcv4, send5, rcv5,
     nb_send, nb_rcv, nb_low, nb_low_rcv, acc1, acc2, part, colsum, secsum, secpart,
     load_sem, small_sem,
-    int_ssem, int_rsem, nb_ssem, nb_rsem, a_ssem, a_rsem, r_ssem, r_rsem,
+    nb_ssem, nb_rsem, a_ssem, a_rsem, r_ssem, r_rsem,
     low_ssem, low_rsem,
 ):
     me = lax.axis_index("sector")
@@ -112,9 +116,32 @@
 
     barrier = pltpu.get_barrier_semaphore()
 
+    rings = ns // 4
+    half = ns // 2
+    wide = nc // 2
+    core, along, high = lax.rem(me, 2), lax.rem(me // 2, rings), me // half
+    across, lane = mycol // 2, lax.rem(mycol, 2)
+
+    def peer(i):
+        step, rest = far_first(i // 4, rings), lax.rem(i, 4)
+        return (
+            lax.rem(high + 1 - rest // 2, 2) * half
+            + lax.rem(along + step, rings) * 2
+            + lax.rem(core + 1 - lax.rem(rest, 2), 2)
+        )
+
+    def low_peer(i):
+        step = far_first(i // 2, rings)
+        return lax.rem(along + step, rings) * 2 + lax.rem(core + 1 - lax.rem(i, 2), 2)
+
+    def high_peer(i):
+        step, rest = far_first(i // 4, wide), lax.rem(i, 4)
+        to = lax.rem(across + step, wide) * 2 + lax.rem(lane + 1 - lax.rem(rest, 2), 2)
+        return lax.rem(high + 1 - rest // 2, 2), to
+
     def greet_sector(i, carry):
         pl.semaphore_signal(
-            barrier, inc=1, device_id={"sector": lax.rem(me + i, ns)}, device_id_type=MESH
+            barrier, inc=1, device_id={"sector": peer(i)}, device_id_type=MESH
         )
         return carry
 
@@ -143,21 +170,20 @@
     ]
     for copy in loads:
         copy.start()
+    lax.fori_loop(0, ns - 1, greet_sector, 0)
+    lax.fori_loop(1, nc, greet_other, 0)
+    lax.fori_loop(1, nc, greet_col, 0)
     smalls = [
         pltpu.make_async_copy(src, dst, small_sem.at[n])
         for n, (src, dst) in enumerate(
-            [(cl_hbm, cl), (cm_hbm, cm), (cr_hbm, cr), (slot_hbm, slot), (stiff_hbm, stiff)]
+            [(cl_hbm, cl), (cm_hbm, cm), (cr_hbm, cr), (stiff_hbm, stiff), (slot_hbm, slot)]
         )
     ]
     for copy in smalls:
         copy.start()
-    for to in (prv, nxt):
-        pl.semaphore_signal(barrier, inc=1, device_id={"sector": to}, device_id_type=MESH)
-    lax.fori_loop(2, ns - 1, greet_sector, 0)
-    lax.fori_loop(1, nc, greet_col, 0)
-    lax.fori_loop(1, nc, greet_other, 0)
     coef_load = pltpu.make_async_copy(coef_hbm, coef, load_sem.at[4])
     coef_load.start()
+
     def combine(i, carry):
         at = pl.ds(pl.multiple_of(i * block, block), block)
         p = [xs[2 * j, at, :] for j in range(4)]
@@ -206,20 +232,43 @@
             for side, to in ((0, prv), (1, nxt))
         ]
 
+    def row_k(s):
+        mask = cm[pl.ds(s, 1), :]
+        return jnp.where(mask == 1, k_stick, jnp.where(mask == 2, k_slip, 0.0))
+
+    def edge_rows(first, last):
+        depth = first.shape[1]
+        k = row_k(LOCAL - 1)
+        return (
+            dot(first, ends[0, 0:depth, :]).astype(BF16),
+            (dot(last, ends[1, 0:depth, :]) * k).astype(BF16),
+        )
+
     def fill_edges(field, ref):
-        nb_send[0, field] = sector_rows(ref, 0).astype(BF16)
-        nb_send[1, field] = sector_rows(ref, LOCAL - 1).astype(BF16)
+        k = jnp.broadcast_to(row_k(LOCAL - 1), (16, 128)).astype(BF16)
+        values = edge_rows(
+            sector_rows(ref, 0).astype(BF16), sector_rows(ref, LOCAL - 1).astype(BF16)
+        )
+        for side in range(2):
+            nb_send[side, field] = jnp.concatenate([values[side], k], axis=0)
+
+    def from_edges(after, before):
+        none = jnp.zeros((cols, 128), BF16)
+        after = (after.astype(F32) * row_k(LOCAL - 1)).astype(BF16)
+        return (
+            jnp.concatenate([after, none], axis=1), jnp.concatenate([before, none], axis=1)
+        )
 
     def send_all(src, dst, stage, ssem, rsem):
         def one(i, carry):
-            to = lax.rem(me + i, ns)
+            to = peer(i)
             pltpu.make_async_remote_copy(
                 src.at[to], dst.at[me], ssem.at[stage], rsem.at[stage],
                 device_id={"sector": to}, device_id_type=MESH,
             ).start()
             return carry
 
-        lax.fori_loop(1, ns, one, 0)
+        lax.fori_loop(0, ns - 1, one, 0)
         dst[me] = src[me]
 
     def wait_all(src, dst, stage, ssem, rsem):
@@ -229,34 +278,7 @@
             device_id={"sector": nxt}, device_id_type=MESH,
         )
 
-    fill_edges(0, yp0)
     for copy in smalls:
-        copy.wait()
-    int_copies = [
-        pltpu.make_async_remote_copy(
-            src, dst, int_ssem.at[n], int_rsem.at[n],
-            device_id={"sector": to}, device_id_type=MESH,
-        )
-        for n, (src, dst, to) in enumerate([(cl, cl_n, nxt), (cm, cm_n, nxt), (cr, cr_n, prv)])
-    ]
-    edge0, edge1, edge2 = [neighbour_copies(field) for field in range(3)]
-
-    pl.semaphore_wait(barrier, ns + 2 * nc - 3)
-
-    for copy in int_copies + edge0:
-        copy.start()
-    send_all(send1, rcv1, 0, a_ssem, a_rsem)
-    fill_edges(1, yp1)
-    for copy in edge1:
-        copy.start()
-
-    smat = pltpu.roll(
-        jnp.broadcast_to(slot[...].astype(F32), (sectors, sectors)), 0, 1, stride=1, stride_axis=0
-    )
-    for k in range(TABLES):
-        picks[:, k * sectors:(k + 1) * sectors] = jnp.where(smat == float(k), 1.0, 0.0).astype(BF16)
-
-    for copy in int_copies:
         copy.wait()
     dof = lax.broadcasted_iota(jnp.int32, (DOF, 128), 0)
     mats_tri = jnp.where(
@@ -268,32 +290,48 @@
         coupling,
         0.0,
     ).astype(BF16)
-    diag = [None] * LOCAL
-    for j in range(LOCAL + 1):
-        left_ref, mask_ref, lrow = (cl_n, cm_n, LOCAL - 1) if j == 0 else (cl, cm, j - 1)
-        right_ref, rrow = (cr_n, 0) if j == LOCAL else (cr, j)
-        left = left_ref[pl.ds(lrow, 1), :]
-        mask = mask_ref[pl.ds(lrow, 1), :]
-        right = right_ref[pl.ds(rrow, 1), :]
-        k = jnp.where(mask == 1, k_stick, jnp.where(mask == 2, k_slip, 0.0))
-        at_left = jnp.where(dof == left, 1.0, 0.0).astype(BF16)
-        at_right = jnp.where(dof == right, 1.0, 0.0).astype(BF16)
-        k_left = jnp.where(dof == left, jnp.broadcast_to(k, (DOF, 128)), 0.0).astype(BF16)
-        k8 = jnp.broadcast_to(k, (8, 128)).astype(BF16)
-        if j > 0:
-            mats[j - 1, 0:DOF, :] = dot(at_right, k_left, (1, 1)).astype(BF16)
-            more = dot(k8, at_left, (1, 1))
-            diag[j - 1] = more if diag[j - 1] is None else diag[j - 1] + more
-        if j < LOCAL:
-            mats[j, DOF:2 * DOF, :] = dot(k_left, at_right, (1, 1)).astype(BF16)
-            mats[j, 2 * DOF:3 * DOF, :] = mats_tri
-            diag[j] = dot(k8, at_right, (1, 1))
+    eye = jnp.where(
+        lax.broadcasted_iota(jnp.int32, (128, 128), 0)
+        == lax.broadcasted_iota(jnp.int32, (128, 128), 1),
+        1.0,
+        0.0,
+    ).astype(BF16)
     row8 = lax.broadcasted_iota(jnp.int32, (8, 128), 0)
     total_k = stiff[...]
     for s in range(LOCAL):
-        total_k = total_k + jnp.where(row8 == s, diag[s][:, 0:128], 0.0)
-        total_k = total_k + jnp.where(row8 == LOCAL + s, diag[s][:, 128:256], 0.0)
-    keff[...] = total_k
+        k = row_k(s)
+        left = cl[pl.ds(s, 1), :]
+        right = cr[pl.ds(s, 1), :]
+        at_left = jnp.where(dof == left, 1.0, 0.0).astype(BF16)
+        at_right = jnp.where(dof == right, 1.0, 0.0).astype(BF16)
+        more = dot(jnp.broadcast_to(k, (8, 128)).astype(BF16), at_left, (1, 1))
+        if s > 0:
+            mats[s - 1, 0:DOF, :] = dot(at_right, k_left, (1, 1)).astype(BF16)
+            mats[s, DOF:2 * DOF, :] = dot(k_left, at_right, (1, 1)).astype(BF16)
+            before = jnp.broadcast_to(row_k(s - 1), (8, 128)).astype(BF16)
+            more = more + dot(before, at_right, (1, 1))
+        else:
+            ends[0] = at_right
+            mats[0, DOF:DOF + 128, :] = dot(eye, at_right, (1, 1)).astype(BF16)
+            mats[0, DOF + 128:2 * DOF, :] = jnp.zeros((128, DOF), BF16)
+        if s == LOCAL - 1:
+            ends[1] = at_left
+            mats[s, 0:128, :] = dot(eye, at_left, (1, 1)).astype(BF16)
+            mats[s, 128:DOF, :] = jnp.zeros((128, DOF), BF16)
+        mats[s, 2 * DOF:3 * DOF, :] = mats_tri
+        total_k = total_k + jnp.where(row8 == s, more[:, 0:128], 0.0)
+        total_k = total_k + jnp.where(row8 == LOCAL + s, more[:, 128:256], 0.0)
+        k_left = jnp.where(dof == left, jnp.broadcast_to(k, (DOF, 128)), 0.0).astype(BF16)
+
+    fill_edges(0, yp0)
+    edge0, edge1, edge2 = [neighbour_copies(field) for field in range(3)]
+
+    pl.semaphore_wait(barrier, ns + 2 * nc - 3)
+
+    for copy in edge0:
+        copy.start()
+    send_all(send1, rcv1, 0, a_ssem, a_rsem)
+    fill_edges(1, yp1)
 
     def cross(own, next_first, prev_last, dst):
         chain = [prev_last] + own + [next_first]
@@ -303,20 +341,21 @@
             dst[pl.ds(s, cols, stride=8), :] = out[:, 0:128]
             dst[pl.ds(4 + s, cols, stride=8), :] = out[:, 128:256]
 
+    def edges_in(field):
+        return from_edges(nb_rcv[0, field, 0:cols, :], nb_rcv[1, field, 0:cols, :])
+
     def cross_of(field, ref, dst):
-        cross(
-            [sector_rows(ref, s).astype(BF16) for s in range(LOCAL)],
-            nb_rcv[0, field], nb_rcv[1, field], dst,
-        )
+        cross([sector_rows(ref, s).astype(BF16) for s in range(LOCAL)], *edges_in(field), dst)
 
     def fine_cross_of(field, ref, dst):
         none = jnp.zeros((cols, DOF), BF16)
-        chain = [jnp.concatenate([nb_rcv[1, field], none], axis=0)]
+        after, before = edges_in(field)
+        chain = [jnp.concatenate([before, none], axis=0)]
         for s in range(LOCAL):
             value = sector_rows(ref, s)
             high = value.astype(BF16)
             chain.append(jnp.concatenate([high, (value - high.astype(F32)).astype(BF16)], axis=0))
-        chain.append(jnp.concatenate([nb_rcv[0, field], none], axis=0))
+        chain.append(jnp.concatenate([after, none], axis=0))
         for s in range(LOCAL):
             both = dot(jnp.concatenate([chain[s + 2], chain[s], chain[s + 1]], axis=1), mats[s])
             out = both[0:cols] + both[cols:2 * cols]
@@ -329,6 +368,9 @@
 
     for copy in edge0:
         copy.wait()
+    more = dot(nb_rcv[1, 0, cols:cols + 16, :], ends[0], (1, 1))[0:8]
+    total_k = total_k + jnp.where(row8 == 0, more[:, 0:128], 0.0)
+    keff[...] = total_k + jnp.where(row8 == LOCAL, more[:, 128:256], 0.0)
     cross_of(0, yp0, cross0)
 
     def second(i, carry):
@@ -348,8 +390,14 @@
     lax.fori_loop(0, blocks, second, 0)
     send_all(send2, rcv2, 1, a_ssem, a_rsem)
     fill_edges(2, yp2)
-    for copy in edge2:
+    for copy in edge1 + edge2:
         copy.start()
+
+    smat = pltpu.roll(
+        jnp.broadcast_to(slot[...].astype(F32), (sectors, sectors)), 0, 1, stride=1, stride_axis=0
+    )
+    for k in range(TABLES):
+        picks[:, k * sectors:(k + 1) * sectors] = jnp.where(smat == float(k), 1.0, 0.0).astype(BF16)
 
     coef_load.wait()
 
@@ -420,8 +468,7 @@
 
     none = jnp.zeros((cols, 128), BF16)
     own = [a0r[pl.ds(s, cols, stride=8), :].astype(BF16) for s in range(LOCAL)]
-    nb_low[0] = own[0]
-    nb_low[1] = own[LOCAL - 1]
+    nb_low[0], nb_low[1] = edge_rows(own[0], own[LOCAL - 1])
     edge_low = [
         pltpu.make_async_remote_copy(
             nb_low.at[side], nb_low_rcv.at[side], low_ssem.at[side], low_rsem.at[side],
@@ -447,8 +494,7 @@
         copy.wait()
     cross(
         [jnp.concatenate([v, none], axis=1) for v in own],
-        jnp.concatenate([nb_low_rcv[0], none], axis=1),
-        jnp.concatenate([nb_low_rcv[1], none], axis=1),
+        *from_edges(nb_low_rcv[0], nb_low_rcv[1]),
         cross0,
     )
 
@@ -472,20 +518,19 @@
 
     part[...] = jnp.sum(squares, axis=0, keepdims=True)
 
-    half = ns // 2
-    low, high = lax.rem(me, half), me // half
+    low = lax.rem(me, half)
     spot = high * nc + mycol
 
     def over_high(i, carry):
-        to = lax.rem(spot + i, 2 * nc)
+        to_high, to = high_peer(i)
         pltpu.make_async_remote_copy(
             part, colsum.at[spot], a_ssem.at[2], a_rsem.at[2],
-            device_id={"sector": low + half * (to // nc), "col": lax.rem(to, nc)},
+            device_id={"sector": low + half * to_high, "col": to},
             device_id_type=MESH,
         ).start()
         return carry
 
-    lax.fori_loop(1, 2 * nc, over_high, 0)
+    lax.fori_loop(0, 2 * nc - 1, over_high, 0)
     colsum[spot] = part[...]
     most = pl.ds(0, 2 * nc - 1)
     pltpu.make_async_remote_copy(
@@ -495,14 +540,14 @@
     secpart[...] = jnp.sum(colsum[...], axis=0)
 
     def over_low(i, carry):
-        to = lax.rem(low + i, half)
+        to = low_peer(i)
         pltpu.make_async_remote_copy(
             secpart, secsum.at[low], r_ssem.at[2], r_rsem.at[2],
             device_id={"sector": high * half + to}, device_id_type=MESH,
         ).start()
         return carry
 
-    lax.fori_loop(1, half, over_low, 0)
+    lax.fori_loop(0, half - 1, over_low, 0)
     secsum[low] = secpart[...]
     most_low = pl.ds(0, half - 1)
     pltpu.make_async_remote_copy(
@@ -539,9 +584,10 @@
             vm((8, 128), F32),
             vm((TABLES * AERO, AERO), BF16),
             vm((1, sectors), jnp.int32),
-            ints, ints, ints, ints, ints, ints,
+            ints, ints, ints,
             vm((8, 128), F32),
             vm((LOCAL, 3 * DOF, DOF), BF16),
+            vm((2, DOF, 128), BF16),
             vm((sectors, TABLES * sectors), BF16),
             vm((TABLES * sectors, 2 * AERO), BF16),
             big, big, big, big, big, big, big,
@@ -551,7 +597,7 @@
             vm((ns, 8, 128), BF16), vm((ns, 8, 128), BF16),
             vm((ns, 8, 128), BF16), vm((ns, 8, 128), BF16),
             vm((ns, 8, 128), BF16), vm((ns, 8, 128), BF16),
-            vm((2, 3, cols, DOF), BF16), vm((2, 3, cols, DOF), BF16),
+            vm((2, 3, cols + 16, 128), BF16), vm((2, 3, cols + 16, 128), BF16),
             vm((2, cols, 128), BF16), vm((2, cols, 128), BF16),
             vm((sectors, 2 * AERO), F32),
             vm((sectors, 2 * AERO), F32),
@@ -560,7 +606,7 @@
             vm((ns // 2, 1, 128), F32),
             vm((1, 128), F32),
             dma((5,)), dma((5,)),
-            dma((3,)), dma((3,)), dma((2, 3)), dma((2, 3)),
+            dma((2, 3)), dma((2, 3)),
             dma((3,)), dma((3,)), dma((4,)), dma((4,)),
             dma((2,)), dma((2,)),
         ],

time: 43.8 us -> 43.9 us (level)
  no operation moved by 1% of the time
where the time goes in v3:
time: 43.9 us; the launch traced here: 43.8 us
  Pallas kernels  41.1 us (94%)
  between operations  1.81 us (4%)
  other arithmetic  0.87 us (2%)
    pallas_call x1, Pallas kernels, per_device(): pl.pallas_call(functools.partial(kernel, ns, nc, float(2 * cols * nc * se...  41.1 us

profile of v3, /device:TPU:1, one launch (start us, length us, event | category | flops | bytes accessed | tf_op | source)
XLA Modules:
  0.0 43.8 jit_solution(2244797466863733107)
XLA Ops:
  0.6 41.1 %sweep.1 = (f32[2,512,128]{2,1,0:T(8,128)S(1)}, f32[1,128]{1,0:T(1,128)S(1)}) custom-call(f32[8,512,128]{2,1,0:T(8,128)} %bitcast.21, f32[8,128]{1,0:T(8,128)} %bitcast.24, bf16[4096,128]{1,0:T(8,128)(2,1)} %bitcast.22, s32[1,128]{1,0:T(1,128)} %bitcast.25, s32[4,128]{1,0:T(4,128)} %cl_hbm.1, s32[4,128]{1,0:T(4,128)} %cr_hbm.1, s32[4,128]{1,0:T(4,128)} %cm_hbm.1), custom_call_target="tpu_custom_call" | custom-call | tf_op jit(solution)/shard_map/sweep/pallas_call | solution.py:574
  41.8 0.9 %broadcast_divide_fusion = f32[2,512,128]{2,1,0:T(8,128)} fusion(f32[2,512,128]{2,1,0:T(8,128)S(1)} %get-tuple-element.4, f32[]{:T(128)S(1)} %bitcast.19), kind=kLoop, calls=%fused_computation | loop fusion | flops 131072 | bytes 1048580 | tf_op jit(solution)/shard_map/div | solution.py:622

commit v4 on v3

--- a/solution.py
+++ b/solution.py
@@ -95,10 +95,10 @@
     x_hbm, stiff_hbm, coef_hbm, slot_hbm, cl_hbm, cr_hbm, cm_hbm,
     st, growth_ref,
     xs, stiff, coef, slot, cl, cr, cm,
-    keff, mats, ends, picks, tabled,
+    keff, extra_k, mats, ends, picks, tabled,
     yp0, yp1, yp2, a0r, cross0, cross1, cross2,
     w_acc, p_acc, e1, e2p, e2w,
-    send1, rcv1, send2, rcv2, send3, rcv3, send4, rcv4, send5, rcv5,
+    send1, rcv1, send2, rcv2, send3, rcv3, send4, rcv4,
     nb_send, nb_rcv, nb_low, nb_low_rcv, acc1, acc2, part, colsum, secsum, secpart,
     load_sem, small_sem,
     nb_ssem, nb_rsem, a_ssem, a_rsem, r_ssem, r_rsem,
@@ -159,6 +159,14 @@
         )
         return carry
 
+    smalls = [
+        pltpu.make_async_copy(src, dst, small_sem.at[n])
+        for n, (src, dst) in enumerate(
+            [(cl_hbm, cl), (cm_hbm, cm), (cr_hbm, cr), (stiff_hbm, stiff), (slot_hbm, slot)]
+        )
+    ]
+    for copy in smalls:
+        copy.start()
     quarter = rows // 4
     loads = [
         pltpu.make_async_copy(
@@ -173,112 +181,14 @@
     lax.fori_loop(0, ns - 1, greet_sector, 0)
     lax.fori_loop(1, nc, greet_other, 0)
     lax.fori_loop(1, nc, greet_col, 0)
-    smalls = [
-        pltpu.make_async_copy(src, dst, small_sem.at[n])
-        for n, (src, dst) in enumerate(
-            [(cl_hbm, cl), (cm_hbm, cm), (cr_hbm, cr), (stiff_hbm, stiff), (slot_hbm, slot)]
-        )
-    ]
-    for copy in smalls:
-        copy.start()
     coef_load = pltpu.make_async_copy(coef_hbm, coef, load_sem.at[4])
     coef_load.start()
-
-    def combine(i, carry):
-        at = pl.ds(pl.multiple_of(i * block, block), block)
-        p = [xs[2 * j, at, :] for j in range(4)]
-        w = [xs[2 * j + 1, at, :] for j in range(4)]
-
-        def quad(m, v):
-            out = v[0] * float(S[m][0])
-            for j in range(1, 4):
-                out = out + float(S[m][j]) * v[j]
-            return out
-
-        y0 = quad(0, p)
-        v0 = quad(0, w)
-        p1 = p[0] + v0
-        y1 = quad(1, p) + H1 * (p1 - p[1])
-        yp0[at, :] = y0
-        yp1[at, :] = y1
-        p_acc[at, :] = p1
-        w_acc[at, :] = w[0] - damping * v0
-        e1[at, :] = quad(1, w) - H1 * w[1]
-        e2p[at, :] = quad(2, p) - H2 * p[2]
-        e2w[at, :] = quad(2, w) - H2 * w[2]
-        chunk = jnp.concatenate(
-            [low_of_pairs(y0), low_of_pairs(C3 * y0 + H2 * y1)], axis=2
-        ).astype(BF16)
-        per = block // 16
-        send1[pl.ds(i * per, per)] = chunk
-        return carry
-
-    for n in range(4):
-        loads[n].wait()
-        lax.fori_loop(n * blocks // 4, (n + 1) * blocks // 4, combine, 0)
-
-    def sector_rows(ref, s):
-        return jnp.concatenate(
-            [ref[pl.ds(s, cols, stride=8), :], ref[pl.ds(4 + s, cols, stride=8), :]], axis=1
-        )
-
-    def neighbour_copies(field):
-        return [
-            pltpu.make_async_remote_copy(
-                nb_send.at[side, field], nb_rcv.at[side, field],
-                nb_ssem.at[side, field], nb_rsem.at[side, field],
-                device_id={"sector": to}, device_id_type=MESH,
-            )
-            for side, to in ((0, prv), (1, nxt))
-        ]
 
     def row_k(s):
         mask = cm[pl.ds(s, 1), :]
         return jnp.where(mask == 1, k_stick, jnp.where(mask == 2, k_slip, 0.0))
 
-    def edge_rows(first, last):
-        depth = first.shape[1]
-        k = row_k(LOCAL - 1)
-        return (
-            dot(first, ends[0, 0:depth, :]).astype(BF16),
-            (dot(last, ends[1, 0:depth, :]) * k).astype(BF16),
-        )
-
-    def fill_edges(field, ref):
-        k = jnp.broadcast_to(row_k(LOCAL - 1), (16, 128)).astype(BF16)
-        values = edge_rows(
-            sector_rows(ref, 0).astype(BF16), sector_rows(ref, LOCAL - 1).astype(BF16)
-        )
-        for side in range(2):
-            nb_send[side, field] = jnp.concatenate([values[side], k], axis=0)
-
-    def from_edges(after, before):
-        none = jnp.zeros((cols, 128), BF16)
-        after = (after.astype(F32) * row_k(LOCAL - 1)).astype(BF16)
-        return (
-            jnp.concatenate([after, none], axis=1), jnp.concatenate([before, none], axis=1)
-        )
-
-    def send_all(src, dst, stage, ssem, rsem):
-        def one(i, carry):
-            to = peer(i)
-            pltpu.make_async_remote_copy(
-                src.at[to], dst.at[me], ssem.at[stage], rsem.at[stage],
-                device_id={"sector": to}, device_id_type=MESH,
-            ).start()
-            return carry
-
-        lax.fori_loop(0, ns - 1, one, 0)
-        dst[me] = src[me]
-
-    def wait_all(src, dst, stage, ssem, rsem):
-        most = pl.ds(0, ns - 1)
-        return pltpu.make_async_remote_copy(
-            src.at[most], dst.at[most], ssem.at[stage], rsem.at[stage],
-            device_id={"sector": nxt}, device_id_type=MESH,
-        )
-
-    for copy in smalls:
+    for copy in smalls[0:4]:
         copy.wait()
     dof = lax.broadcasted_iota(jnp.int32, (DOF, 128), 0)
     mats_tri = jnp.where(
@@ -322,6 +232,95 @@
         total_k = total_k + jnp.where(row8 == s, more[:, 0:128], 0.0)
         total_k = total_k + jnp.where(row8 == LOCAL + s, more[:, 128:256], 0.0)
         k_left = jnp.where(dof == left, jnp.broadcast_to(k, (DOF, 128)), 0.0).astype(BF16)
+    keff[...] = total_k
+
+    def combine(i, carry):
+        at = pl.ds(pl.multiple_of(i * block, block), block)
+        p = [xs[2 * j, at, :] for j in range(4)]
+        w = [xs[2 * j + 1, at, :] for j in range(4)]
+
+        def quad(m, v):
+            out = v[0] * float(S[m][0])
+            for j in range(1, 4):
+                out = out + float(S[m][j]) * v[j]
+            return out
+
+        y0 = quad(0, p)
+        v0 = quad(0, w)
+        p1 = p[0] + v0
+        y1 = quad(1, p) + H1 * (p1 - p[1])
+        yp0[at, :] = y0
+        yp1[at, :] = y1
+        p_acc[at, :] = p1
+        w_acc[at, :] = w[0] - damping * v0
+        e1[at, :] = quad(1, w) - H1 * w[1]
+        e2p[at, :] = quad(2, p) - H2 * p[2]
+        e2w[at, :] = quad(2, w) - H2 * w[2]
+        per = block // 16
+        send1[pl.ds(i * per, per), :, 0:128] = low_of_pairs(y0).astype(BF16)
+        send1[pl.ds(i * per, per), :, 128:256] = low_of_pairs(C3 * y0 + H2 * y1).astype(BF16)
+        return carry
+
+    for n in range(4):
+        loads[n].wait()
+        lax.fori_loop(n * blocks // 4, (n + 1) * blocks // 4, combine, 0)
+
+    def sector_rows(ref, s):
+        return jnp.concatenate(
+            [ref[pl.ds(s, cols, stride=8), :], ref[pl.ds(4 + s, cols, stride=8), :]], axis=1
+        )
+
+    def neighbour_copies(field):
+        return [
+            pltpu.make_async_remote_copy(
+                nb_send.at[side, field], nb_rcv.at[side, field],
+                nb_ssem.at[side, field], nb_rsem.at[side, field],
+                device_id={"sector": to}, device_id_type=MESH,
+            )
+            for side, to in ((0, prv), (1, nxt))
+        ]
+
+    def edge_rows(first, last):
+        depth = first.shape[1]
+        k = row_k(LOCAL - 1)
+        return (
+            dot(first, ends[0, 0:depth, :]).astype(BF16),
+            (dot(last, ends[1, 0:depth, :]) * k).astype(BF16),
+        )
+
+    def fill_edges(field, ref):
+        k = jnp.broadcast_to(row_k(LOCAL - 1), (16, 128)).astype(BF16)
+        values = edge_rows(
+            sector_rows(ref, 0).astype(BF16), sector_rows(ref, LOCAL - 1).astype(BF16)
+        )
+        for side in range(2):
+            nb_send[side, field] = jnp.concatenate([values[side], k], axis=0)
+
+    def from_edges(after, before):
+        none = jnp.zeros((cols, 128), BF16)
+        after = (after.astype(F32) * row_k(LOCAL - 1)).astype(BF16)
+        return (
+            jnp.concatenate([after, none], axis=1), jnp.concatenate([before, none], axis=1)
+        )
+
+    def send_all(src, dst, stage, ssem, rsem):
+        def one(i, carry):
+            to = peer(i)
+            pltpu.make_async_remote_copy(
+                src.at[to], dst.at[me], ssem.at[stage], rsem.at[stage],
+                device_id={"sector": to}, device_id_type=MESH,
+            ).start()
+            return carry
+
+        lax.fori_loop(0, ns - 1, one, 0)
+        dst[me] = src[me]
+
+    def wait_all(src, dst, stage, ssem, rsem):
+        most = pl.ds(0, ns - 1)
+        return pltpu.make_async_remote_copy(
+            src.at[most], dst.at[most], ssem.at[stage], rsem.at[stage],
+            device_id={"sector": nxt}, device_id_type=MESH,
+        )
 
     fill_edges(0, yp0)
     edge0, edge1, edge2 = [neighbour_copies(field) for field in range(3)]
@@ -343,9 +342,6 @@
 
     def edges_in(field):
         return from_edges(nb_rcv[0, field, 0:cols, :], nb_rcv[1, field, 0:cols, :])
-
-    def cross_of(field, ref, dst):
-        cross([sector_rows(ref, s).astype(BF16) for s in range(LOCAL)], *edges_in(field), dst)
 
     def fine_cross_of(field, ref, dst):
         none = jnp.zeros((cols, DOF), BF16)
@@ -366,12 +362,8 @@
         tiles = rows_value.reshape(rows_value.shape[0] // 8, 8, 128)
         return (tiles * keff[...][None]).reshape(rows_value.shape)
 
-    for copy in edge0:
-        copy.wait()
-    more = dot(nb_rcv[1, 0, cols:cols + 16, :], ends[0], (1, 1))[0:8]
-    total_k = total_k + jnp.where(row8 == 0, more[:, 0:128], 0.0)
-    keff[...] = total_k + jnp.where(row8 == LOCAL, more[:, 128:256], 0.0)
-    cross_of(0, yp0, cross0)
+    none = jnp.zeros((cols, DOF), BF16)
+    cross([sector_rows(yp0, s).astype(BF16) for s in range(LOCAL)], none, none, cross0)
 
     def second(i, carry):
         at = pl.ds(pl.multiple_of(i * block, block), block)
@@ -383,16 +375,56 @@
         yp2[at, :] = y2
         p_acc[at, :] = p2
         w_acc[at, :] = w1 - damping * v1
+        cross1[at, :] = C1 * y0 + C2 * yp1[at, :] + y2
+        return carry
+
+    lax.fori_loop(0, blocks, second, 0)
+
+    for copy in edge0:
+        copy.wait()
+    after, before = edges_in(0)
+    out = dot(before[:, 0:128], mats[0, DOF:DOF + 128, :])
+    cross0[pl.ds(0, cols, stride=8), :] = out[:, 0:128]
+    cross0[pl.ds(4, cols, stride=8), :] = out[:, 128:256]
+    out = dot(after[:, 0:128], mats[LOCAL - 1, 0:128, :])
+    cross0[pl.ds(LOCAL - 1, cols, stride=8), :] = out[:, 0:128]
+    cross0[pl.ds(4 + LOCAL - 1, cols, stride=8), :] = out[:, 128:256]
+    more = dot(nb_rcv[1, 0, cols:cols + 16, :], ends[0], (1, 1))[0:8]
+    extra_k[...] = jnp.where(row8 == 0, more[:, 0:128], 0.0) + jnp.where(
+        row8 == LOCAL, more[:, 128:256], 0.0
+    )
+    place = lax.broadcasted_iota(jnp.int32, (block // 8, 8, 128), 1) % LOCAL
+    outer = (place == 0) | (place == LOCAL - 1)
+
+    def correction(at):
+        shape = (block // 8, 8, 128)
+        value = jnp.where(outer, cross0[at, :].reshape(shape), 0.0)
+        return (value - extra_k[...][None] * yp0[at, :].reshape(shape)).reshape(block, 128)
+
+    def correct_v(i, carry):
+        at = pl.ds(pl.multiple_of(i * block, block), block)
         per = block // 16
-        send2[pl.ds(i * per, per)] = low_of_pairs(C1 * y0 + C2 * yp1[at, :] + y2).astype(BF16)
-        return carry
-
-    lax.fori_loop(0, blocks, second, 0)
+        send2[pl.ds(i * per, per)] = low_of_pairs(cross1[at, :] + HH * correction(at)).astype(BF16)
+        return carry
+
+    lax.fori_loop(0, blocks, correct_v, 0)
     send_all(send2, rcv2, 1, a_ssem, a_rsem)
+
+    def correct_rest(i, carry):
+        at = pl.ds(pl.multiple_of(i * block, block), block)
+        change = correction(at)
+        yp2[at, :] = yp2[at, :] + HH * change
+        p_acc[at, :] = p_acc[at, :] + H1 * change
+        w_acc[at, :] = w_acc[at, :] + (1.0 - damping * H1) * change
+        return carry
+
+    lax.fori_loop(0, blocks, correct_rest, 0)
+    keff[...] = keff[...] + extra_k[...]
     fill_edges(2, yp2)
     for copy in edge1 + edge2:
         copy.start()
 
+    smalls[4].wait()
     smat = pltpu.roll(
         jnp.broadcast_to(slot[...].astype(F32), (sectors, sectors)), 0, 1, stride=1, stride_axis=0
     )
@@ -403,7 +435,7 @@
 
     def loads_of(surfaces, acc):
         parts = len(surfaces)
-        lhs = jnp.concatenate(surfaces, axis=0).astype(BF16)
+        lhs = jnp.concatenate(list(surfaces), axis=0).astype(BF16)
         for k in range(0, TABLES, 2):
             u = dot(lhs, coef[k * AERO:(k + 2) * AERO, :], (1, 1)).astype(BF16)
             for n in range(2):
@@ -426,12 +458,19 @@
 
     wait_all(send1, rcv1, 0, a_ssem, a_rsem).wait()
     arrived = by_sector(rcv1[...])
-    loads_of([arrived[c][:, 0:AERO] for c in range(2)], acc1)
-    send3[...] = by_device(acc1[:, 0:AERO], acc1[:, AERO:2 * AERO]).astype(BF16)
+    loads_of([arrived[c][:, f * AERO:(f + 1) * AERO] for f in range(2) for c in range(2)], acc2)
+    for n in range(2):
+        at = 2 * n * AERO
+        send3[:, :, n * AERO:(n + 1) * AERO] = by_device(
+            acc2[:, at:at + AERO], acc2[:, at + AERO:at + 2 * AERO]
+        ).astype(BF16)
     send_all(send3, rcv3, 0, r_ssem, r_rsem)
-    loads_of([arrived[c][:, AERO:2 * AERO] for c in range(2)], acc2)
-    send5[...] = by_device(acc2[:, 0:AERO], acc2[:, AERO:2 * AERO]).astype(BF16)
-    send_all(send5, rcv5, 3, r_ssem, r_rsem)
+
+    wait_all(send2, rcv2, 1, a_ssem, a_rsem).wait()
+    rest = by_sector(rcv2[...])
+    loads_of([rest[c] + HH * acc2[:, c * AERO:(c + 1) * AERO] for c in range(2)], acc1)
+    send4[...] = by_device(acc1[:, 0:AERO], acc1[:, AERO:2 * AERO]).astype(BF16)
+    send_all(send4, rcv4, 1, r_ssem, r_rsem)
 
     for copy in edge1 + edge2:
         copy.wait()
@@ -448,23 +487,18 @@
 
     lax.fori_loop(0, blocks, third, 0)
 
-    wait_all(send2, rcv2, 1, a_ssem, a_rsem).wait()
-    rest = by_sector(rcv2[...])
-    loads_of(
-        [rest[c] + HH * acc1[:, c * AERO:(c + 1) * AERO] for c in range(2)], acc2
-    )
-    send4[...] = by_device(acc2[:, 0:AERO], acc2[:, AERO:2 * AERO]).astype(BF16)
-    send_all(send4, rcv4, 1, r_ssem, r_rsem)
-
     wait_all(send3, rcv3, 0, r_ssem, r_rsem).wait()
 
     def spread(i, carry):
         per = block // 16
         at = pl.ds(pl.multiple_of(i * block, block), block)
-        a0r[at, :] = pairs_of_low(rcv3[pl.ds(i * per, per)].astype(F32))
-        return carry
-
-    lax.fori_loop(0, blocks, spread, 0)
+        got = rcv3[pl.ds(i * per, per)].astype(F32)
+        a0r[at, :] = pairs_of_low(got[:, :, 0:128])
+        p3 = p_acc[at, :] + pairs_of_low(got[:, :, 128:256])
+        st[0, at, :] = p3
+        return carry + jnp.sum((p3 * p3).reshape(block // 8, 8, 128), axis=0)
+
+    squares = lax.fori_loop(0, blocks, spread, jnp.zeros((8, 128), F32))
 
     none = jnp.zeros((cols, 128), BF16)
     own = [a0r[pl.ds(s, cols, stride=8), :].astype(BF16) for s in range(LOCAL)]
@@ -479,17 +513,6 @@
     for copy in edge_low:
         copy.start()
 
-    wait_all(send5, rcv5, 3, r_ssem, r_rsem).wait()
-
-    def close_p(i, carry):
-        per = block // 16
-        at = pl.ds(pl.multiple_of(i * block, block), block)
-        p3 = p_acc[at, :] + pairs_of_low(rcv5[pl.ds(i * per, per)].astype(F32))
-        st[0, at, :] = p3
-        return carry + jnp.sum((p3 * p3).reshape(block // 8, 8, 128), axis=0)
-
-    squares = lax.fori_loop(0, blocks, close_p, jnp.zeros((8, 128), F32))
-
     for copy in edge_low:
         copy.wait()
     cross(
@@ -507,14 +530,14 @@
 
     wait_all(send4, rcv4, 1, r_ssem, r_rsem).wait()
 
-    def fifth(i, carry):
+    def close(i, carry):
         per = block // 16
         at = pl.ds(pl.multiple_of(i * block, block), block)
         w3 = w_acc[at, :] + pairs_of_low(rcv4[pl.ds(i * per, per)].astype(F32))
         st[1, at, :] = w3
         return carry + jnp.sum((w3 * w3).reshape(block // 8, 8, 128), axis=0)
 
-    squares = lax.fori_loop(0, blocks, fifth, squares)
+    squares = lax.fori_loop(0, blocks, close, squares)
 
     part[...] = jnp.sum(squares, axis=0, keepdims=True)
 
@@ -586,28 +609,28 @@
             vm((1, sectors), jnp.int32),
             ints, ints, ints,
             vm((8, 128), F32),
+            vm((8, 128), F32),
             vm((LOCAL, 3 * DOF, DOF), BF16),
             vm((2, DOF, 128), BF16),
             vm((sectors, TABLES * sectors), BF16),
-            vm((TABLES * sectors, 2 * AERO), BF16),
+            vm((TABLES * sectors, 4 * AERO), BF16),
             big, big, big, big, big, big, big,
             big, big, big, big, big,
             vm((ns, 8, 256), BF16), vm((ns, 8, 256), BF16),
             vm((ns, 8, 128), BF16), vm((ns, 8, 128), BF16),
-            vm((ns, 8, 128), BF16), vm((ns, 8, 128), BF16),
-            vm((ns, 8, 128), BF16), vm((ns, 8, 128), BF16),
+            vm((ns, 8, 256), BF16), vm((ns, 8, 256), BF16),
             vm((ns, 8, 128), BF16), vm((ns, 8, 128), BF16),
             vm((2, 3, cols + 16, 128), BF16), vm((2, 3, cols + 16, 128), BF16),
             vm((2, cols, 128), BF16), vm((2, cols, 128), BF16),
             vm((sectors, 2 * AERO), F32),
-            vm((sectors, 2 * AERO), F32),
+            vm((sectors, 4 * AERO), F32),
             vm((1, 128), F32),
             vm((2 * nc, 1, 128), F32),
             vm((ns // 2, 1, 128), F32),
             vm((1, 128), F32),
             dma((5,)), dma((5,)),
             dma((2, 3)), dma((2, 3)),
-            dma((3,)), dma((3,)), dma((4,)), dma((4,)),
+            dma((3,)), dma((3,)), dma((3,)), dma((3,)),
             dma((2,)), dma((2,)),
         ],
         compiler_params=pltpu.CompilerParams(

time: 43.9 us -> 42.3 us (0.964)
  Pallas kernels: 41.1 us -> 39.6 us
    pallas_call x1, Pallas kernels: 41.1 us -> 39.6 us  [per_device(): pl.pallas_call(functools.partial(kernel, ns, nc, float(2 * cols * nc * se...]
where the time goes in v4:
time: 42.3 us; the launch traced here: 42.2 us
  Pallas kernels  39.6 us (94%)
  between operations  1.81 us (4%)
  other arithmetic  0.87 us (2%)
    pallas_call x1, Pallas kernels, per_device(): pl.pallas_call(functools.partial(kernel, ns, nc, float(2 * cols * nc * se...  39.6 us
    div x1, other arithmetic, per_device(): scaled = state / value  0.87 us

profile of v4, /device:TPU:1, one launch (start us, length us, event | category | flops | bytes accessed | tf_op | source)
XLA Modules:
  0.0 42.2 jit_solution(1672685416184846164)
XLA Ops:
  0.6 39.6 %sweep.1 = (f32[2,512,128]{2,1,0:T(8,128)S(1)}, f32[1,128]{1,0:T(1,128)S(1)}) custom-call(f32[8,512,128]{2,1,0:T(8,128)} %bitcast.21, f32[8,128]{1,0:T(8,128)} %bitcast.24, bf16[4096,128]{1,0:T(8,128)(2,1)} %bitcast.22, s32[1,128]{1,0:T(1,128)} %bitcast.25, s32[4,128]{1,0:T(4,128)} %cl_hbm.1, s32[4,128]{1,0:T(4,128)} %cr_hbm.1, s32[4,128]{1,0:T(4,128)} %cm_hbm.1), custom_call_target="tpu_custom_call" | custom-call | tf_op jit(solution)/shard_map/sweep/pallas_call | solution.py:597
  40.2 0.9 %broadcast_divide_fusion = f32[2,512,128]{2,1,0:T(8,128)} fusion(f32[2,512,128]{2,1,0:T(8,128)S(1)} %get-tuple-element.4, f32[]{:T(128)S(1)} %bitcast.19), kind=kLoop, calls=%fused_computation | loop fusion | flops 131072 | bytes 1048580 | tf_op jit(solution)/shard_map/div | solution.py:645

commit v5 on v4

--- a/solution.py
+++ b/solution.py
@@ -234,6 +234,13 @@
         k_left = jnp.where(dof == left, jnp.broadcast_to(k, (DOF, 128)), 0.0).astype(BF16)
     keff[...] = total_k
 
+    smalls[4].wait()
+    smat = pltpu.roll(
+        jnp.broadcast_to(slot[...].astype(F32), (sectors, sectors)), 0, 1, stride=1, stride_axis=0
+    )
+    for k in range(TABLES):
+        picks[:, k * sectors:(k + 1) * sectors] = jnp.where(smat == float(k), 1.0, 0.0).astype(BF16)
+
     def combine(i, carry):
         at = pl.ds(pl.multiple_of(i * block, block), block)
         p = [xs[2 * j, at, :] for j in range(4)]
@@ -330,7 +337,6 @@
     for copy in edge0:
         copy.start()
     send_all(send1, rcv1, 0, a_ssem, a_rsem)
-    fill_edges(1, yp1)
 
     def cross(own, next_first, prev_last, dst):
         chain = [prev_last] + own + [next_first]
@@ -420,16 +426,10 @@
 
     lax.fori_loop(0, blocks, correct_rest, 0)
     keff[...] = keff[...] + extra_k[...]
+    fill_edges(1, yp1)
     fill_edges(2, yp2)
     for copy in edge1 + edge2:
         copy.start()
-
-    smalls[4].wait()
-    smat = pltpu.roll(
-        jnp.broadcast_to(slot[...].astype(F32), (sectors, sectors)), 0, 1, stride=1, stride_axis=0
-    )
-    for k in range(TABLES):
-        picks[:, k * sectors:(k + 1) * sectors] = jnp.where(smat == float(k), 1.0, 0.0).astype(BF16)
 
     coef_load.wait()
 
@@ -544,40 +544,40 @@
     low = lax.rem(me, half)
     spot = high * nc + mycol
 
+    def over_low(i, carry):
+        to = low_peer(i)
+        pltpu.make_async_remote_copy(
+            part, secsum.at[low], r_ssem.at[2], r_rsem.at[2],
+            device_id={"sector": high * half + to}, device_id_type=MESH,
+        ).start()
+        return carry
+
+    lax.fori_loop(0, half - 1, over_low, 0)
+    secsum[low] = part[...]
+    most_low = pl.ds(0, half - 1)
+    pltpu.make_async_remote_copy(
+        secsum.at[most_low], secsum.at[most_low], r_ssem.at[2], r_rsem.at[2],
+        device_id={"sector": nxt}, device_id_type=MESH,
+    ).wait()
+    secpart[...] = jnp.sum(secsum[...], axis=0)
+
     def over_high(i, carry):
         to_high, to = high_peer(i)
         pltpu.make_async_remote_copy(
-            part, colsum.at[spot], a_ssem.at[2], a_rsem.at[2],
+            secpart, colsum.at[spot], a_ssem.at[2], a_rsem.at[2],
             device_id={"sector": low + half * to_high, "col": to},
             device_id_type=MESH,
         ).start()
         return carry
 
     lax.fori_loop(0, 2 * nc - 1, over_high, 0)
-    colsum[spot] = part[...]
+    colsum[spot] = secpart[...]
     most = pl.ds(0, 2 * nc - 1)
     pltpu.make_async_remote_copy(
         colsum.at[most], colsum.at[most], a_ssem.at[2], a_rsem.at[2],
         device_id={"sector": nxt}, device_id_type=MESH,
     ).wait()
-    secpart[...] = jnp.sum(colsum[...], axis=0)
-
-    def over_low(i, carry):
-        to = low_peer(i)
-        pltpu.make_async_remote_copy(
-            secpart, secsum.at[low], r_ssem.at[2], r_rsem.at[2],
-            device_id={"sector": high * half + to}, device_id_type=MESH,
-        ).start()
-        return carry
-
-    lax.fori_loop(0, half - 1, over_low, 0)
-    secsum[low] = secpart[...]
-    most_low = pl.ds(0, half - 1)
-    pltpu.make_async_remote_copy(
-        secsum.at[most_low], secsum.at[most_low], r_ssem.at[2], r_rsem.at[2],
-        device_id={"sector": nxt}, device_id_type=MESH,
-    ).wait()
-    everything = jnp.sum(jnp.sum(secsum[...], axis=0), axis=1, keepdims=True)
+    everything = jnp.sum(jnp.sum(colsum[...], axis=0), axis=1, keepdims=True)
     growth_ref[...] = jnp.broadcast_to(jnp.sqrt(everything / total_count + 1e-6), (1, 128))
 
 

time: 42.3 us -> 42.2 us (level)
  no operation moved by 1% of the time
where the time goes in v5:
time: 42.2 us; the launch traced here: 42.1 us
  Pallas kernels  39.4 us (93%)
  between operations  1.81 us (4%)
  other arithmetic  0.87 us (2%)
    pallas_call x1, Pallas kernels, per_device(): pl.pallas_call(functools.partial(kernel, ns, nc, float(2 * cols * nc * se...  39.4 us
    div x1, other arithmetic, per_device(): scaled = state / value  0.87 us

profile of v5, /device:TPU:1, one launch (start us, length us, event | category | flops | bytes accessed | tf_op | source)
XLA Modules:
  0.0 42.1 jit_solution(1010781966612708825)
XLA Ops:
  0.6 39.4 %sweep.1 = (f32[2,512,128]{2,1,0:T(8,128)S(1)}, f32[1,128]{1,0:T(1,128)S(1)}) custom-call(f32[8,512,128]{2,1,0:T(8,128)} %bitcast.21, f32[8,128]{1,0:T(8,128)} %bitcast.24, bf16[4096,128]{1,0:T(8,128)(2,1)} %bitcast.22, s32[1,128]{1,0:T(1,128)} %bitcast.25, s32[4,128]{1,0:T(4,128)} %cl_hbm.1, s32[4,128]{1,0:T(4,128)} %cr_hbm.1, s32[4,128]{1,0:T(4,128)} %cm_hbm.1), custom_call_target="tpu_custom_call" | custom-call | tf_op jit(solution)/shard_map/sweep/pallas_call | solution.py:597
  40.0 0.9 %broadcast_divide_fusion = f32[2,512,128]{2,1,0:T(8,128)} fusion(f32[2,512,128]{2,1,0:T(8,128)S(1)} %get-tuple-element.4, f32[]{:T(128)S(1)} %bitcast.19), kind=kLoop, calls=%fused_computation | loop fusion | flops 131072 | bytes 1048580 | tf_op jit(solution)/shard_map/div | solution.py:645

commit v6 on v5

--- a/solution.py
+++ b/solution.py
@@ -178,7 +178,7 @@
     ]
     for copy in loads:
         copy.start()
-    lax.fori_loop(0, ns - 1, greet_sector, 0)
+    lax.fori_loop(0, ns - 1, greet_sector, 0, unroll=True)
     lax.fori_loop(1, nc, greet_other, 0)
     lax.fori_loop(1, nc, greet_col, 0)
     coef_load = pltpu.make_async_copy(coef_hbm, coef, load_sem.at[4])
@@ -319,7 +319,7 @@
             ).start()
             return carry
 
-        lax.fori_loop(0, ns - 1, one, 0)
+        lax.fori_loop(0, ns - 1, one, 0, unroll=True)
         dst[me] = src[me]
 
     def wait_all(src, dst, stage, ssem, rsem):
@@ -552,7 +552,7 @@
         ).start()
         return carry
 
-    lax.fori_loop(0, half - 1, over_low, 0)
+    lax.fori_loop(0, half - 1, over_low, 0, unroll=True)
     secsum[low] = part[...]
     most_low = pl.ds(0, half - 1)
     pltpu.make_async_remote_copy(
@@ -570,7 +570,7 @@
         ).start()
         return carry
 
-    lax.fori_loop(0, 2 * nc - 1, over_high, 0)
+    lax.fori_loop(0, 2 * nc - 1, over_high, 0, unroll=True)
     colsum[spot] = secpart[...]
     most = pl.ds(0, 2 * nc - 1)
     pltpu.make_async_remote_copy(

time: 42.2 us -> 41.9 us (level)
  no operation moved by 1% of the time
where the time goes in v6:
time: 41.9 us; the launch traced here: 41.8 us
  Pallas kernels  39.1 us (93%)
  between operations  1.81 us (4%)
  other arithmetic  0.87 us (2%)
    pallas_call x1, Pallas kernels, per_device(): pl.pallas_call(functools.partial(kernel, ns, nc, float(2 * cols * nc * se...  39.1 us
    div x1, other arithmetic, per_device(): scaled = state / value  0.87 us

profile of v6, /device:TPU:1, one launch (start us, length us, event | category | flops | bytes accessed | tf_op | source)
XLA Modules:
  0.0 41.8 jit_solution(6136392328800191010)
XLA Ops:
  0.6 39.1 %sweep.1 = (f32[2,512,128]{2,1,0:T(8,128)S(1)}, f32[1,128]{1,0:T(1,128)S(1)}) custom-call(f32[8,512,128]{2,1,0:T(8,128)} %bitcast.21, f32[8,128]{1,0:T(8,128)} %bitcast.24, bf16[4096,128]{1,0:T(8,128)(2,1)} %bitcast.22, s32[1,128]{1,0:T(1,128)} %bitcast.25, s32[4,128]{1,0:T(4,128)} %cl_hbm.1, s32[4,128]{1,0:T(4,128)} %cr_hbm.1, s32[4,128]{1,0:T(4,128)} %cm_hbm.1), custom_call_target="tpu_custom_call" | custom-call | tf_op jit(solution)/shard_map/sweep/pallas_call | solution.py:597
  39.7 0.9 %broadcast_divide_fusion = f32[2,512,128]{2,1,0:T(8,128)} fusion(f32[2,512,128]{2,1,0:T(8,128)S(1)} %get-tuple-element.4, f32[]{:T(128)S(1)} %bitcast.19), kind=kLoop, calls=%fused_computation | loop fusion | flops 131072 | bytes 1048580 | tf_op jit(solution)/shard_map/div | solution.py:645
